TPU v7x, 32 devices: a whole 2x2x4 slice. The times are simulated.
32 devices in a mesh: rep: 2 (over y), row: 4 (over x, core), col: 4 (over z).
Axes of the slice: x: 2, y: 2, z: 4, core: 2. Of those that a mesh axis runs over, the one named last changes fastest.
Arguments:
- noise: bfloat16 [16, 4, 4, 1536], P('rep', 'row', 'col'), parts along dimension 0, may hold values from -6 to 6
- block_values: bfloat16 [8, 4, 8, 384, 384], P(('rep', 'row'), 'col'), parts along dimension 0, as said below
- block_rows: int32 [8, 4, 8], P(('rep', 'row'), 'col'), parts along dimension 0, may hold values from 0 to 15
- block_cols: int32 [8, 4, 8], P(('rep', 'row'), 'col'), parts along dimension 0, may hold values from 0 to 15
- block_count: int32 [8, 4], P(('rep', 'row'), 'col'), parts along dimension 0, may hold values from 2 to 8, as said below
- self_mobility: float32 [8, 6144], P(('rep', 'row')), parts along dimension 0, may hold values from 0.4 to 1.6
Outputs:
- first_term: bfloat16 [16, 4, 4, 1536], P('rep', 'col', 'row'), parts along dimension 0
- second_term: bfloat16 [16, 4, 4, 1536], P('rep', 'row', 'col'), parts along dimension 0
There are 2 independent parts, one for each index of `rep`. A program takes and returns all parts, laid end to end along the dimension named above; each array names one. Nothing has to cross between parts.
Inputs may be any that keep to these rules, and one draw needn't show every extreme that they name: block_values, block_rows and block_cols describe a symmetric M: the slot list of owner (i, j) is that of owner (j, i) with rows and columns swapped and blocks transposed, slot by slot; on owners with i = j, slots 2k and 2k + 1 hold a block and its transpose with swapped rows and columns. `block_count`: even, equal on owners (i, j) and (j, i); owners with |i - j| <= 1 have exactly 8 live slots; owners (0, 3) and (3, 0) have exactly 2.
All inputs are finite; a program needn't handle non-finite values.
Results may differ from a plain program's by a relative error of at most 0.014.
Values may be sent and summed in bfloat16 or wider, within the bound.
No kernel may reach another device: no remote copies, remote signals or barrier semaphores. Data moves between devices by JAX's collectives and lax.ppermute only.
A program may use at most 64 MiB of HBM per device.

v0:
```python
import jax
import jax.numpy as jnp
from jax import lax
from jax.sharding import PartitionSpec as P

SHIFT = 1.0
HALF_WIDTH = 0.75


def slot_products(gathered, tiles, read_at, write_at, live_count, transpose):
    vectors, group_len = gathered.shape
    span_len = tiles.shape[-1]
    blocks = group_len // span_len
    grid_view = gathered.reshape(vectors, blocks, span_len)
    picked = grid_view[:, read_at]
    if transpose:
        product = jnp.einsum("vsk,skm->vsm", picked, tiles, preferred_element_type=jnp.float32)
    else:
        product = jnp.einsum("vsk,smk->vsm", picked, tiles, preferred_element_type=jnp.float32)
    slot_ids = jnp.arange(tiles.shape[0], dtype=jnp.int32)
    live_mask = (slot_ids < live_count).astype(jnp.float32)
    placing = (write_at[:, None] == jnp.arange(blocks, dtype=jnp.int32)[None, :]).astype(
        jnp.float32
    )
    placing = placing * live_mask[:, None]
    running = jnp.einsum("vsm,sg->vgm", product, placing, precision=lax.Precision.HIGHEST)
    return running.reshape(vectors, group_len)


def on_device(noise, block_values, block_rows, block_cols, block_count, self_mobility):
    vectors = noise.shape[0]
    tiles = block_values[0, 0]
    rows_here = block_rows[0, 0]
    cols_here = block_cols[0, 0]
    live_count = block_count[0, 0]
    groups = lax.axis_size("row")
    piece_len = noise.shape[3]
    factor = (lax.axis_index("row") == lax.axis_index("col")).astype(jnp.float32)
    self_shift = factor * (self_mobility[0] - SHIFT)
    gathered = lax.all_gather(noise, "col", axis=2, tiled=True).reshape(vectors, -1)
    partial_value = slot_products(gathered, tiles, rows_here, cols_here, live_count, True)
    partial_value = partial_value + self_shift[None, :] * gathered.astype(jnp.float32)
    shares = lax.psum_scatter(
        partial_value.reshape(vectors, 1, groups, piece_len).astype(jnp.bfloat16),
        "row",
        scatter_dimension=2,
        tiled=True,
    ).astype(jnp.float32)
    first_term = (shares / HALF_WIDTH).astype(jnp.bfloat16)
    first_all = lax.all_gather(first_term, "row", axis=2, tiled=True).reshape(vectors, -1)
    second_partial = slot_products(first_all, tiles, cols_here, rows_here, live_count, False)
    second_partial = second_partial + self_shift[None, :] * first_all.astype(jnp.float32)
    second_shares = lax.psum_scatter(
        second_partial.reshape(vectors, 1, groups, piece_len).astype(jnp.bfloat16),
        "col",
        scatter_dimension=2,
        tiled=True,
    ).astype(jnp.float32)
    second_term = (2.0 * second_shares / HALF_WIDTH - noise.astype(jnp.float32)).astype(
        jnp.bfloat16
    )
    return (first_term, second_term)


def solution(mesh):
    placed = (
        P("rep", "row", "col", None),
        P(("rep", "row"), "col", None, None, None),
        P(("rep", "row"), "col", None),
        P(("rep", "row"), "col", None),
        P(("rep", "row"), "col"),
        P(("rep", "row"), None),
    )
    return jax.shard_map(
        on_device,
        mesh=mesh,
        in_specs=placed,
        out_specs=(P("rep", "col", "row", None), P("rep", "row", "col", None)),
        check_vma=False,
    )
```

profile of v0, /device:TPU:0, one launch (start us, length us, event | category | flops | bytes accessed | tf_op | source)
XLA Modules:
  0.0 84.6 jit_solution(15523303134134595494)
XLA Ops:
  7.2 0.0 copy-start
  7.2 0.0 copy-start.2
  7.2 0.0 reduce-scatter.3.cloned.1.call-start
  8.0 0.7 fusion.27
  8.7 0.8 multiply_reduce_fusion
  9.5 15.2 %all_gather.6 = bf16[8,1,4,1536]{3,0,1,2:T(8,128)(2,1)S(1)} all-gather(bf16[8,1,1,1536]{3,0,1,2:T(8,128)(2,1)} %bitcast.52), channel_id=1, replica_groups=mesh['rep'=2,'row'=4,'col'=4] {'col'}, dimensions={2}, use_global_device_ids=true | all-gather | bytes 122880 | tf_op jit(solution)/shard_map/all_gather | solution.py:40
  24.8 0.6 gather_fusion
  25.4 0.0 copy-done
  25.4 0.5 fusion.4
  25.8 0.0 copy-start.3
  25.8 0.0 copy-done.2
  25.8 0.4 convolution_bitcast_fusion.1
  26.3 0.1 reshape.97
  26.4 0.0 copy-start.1
  26.4 0.7 fusion.11
  27.1 0.0 reduce-scatter.3.cloned.1.call-update
  27.1 0.0 reduce-scatter.5.cloned.1.call-start
  27.2 20.7 %reduce-scatter.3.cloned.1.call-done = bf16[8,1,1,1536]{3,0,1,2:T(8,128)(2,1)} async-done(((bf16[8,1,4,1536]{3,0,1,2:T(8,128)(2,1)}), bf16[8,1,1,1536]{3,0,1,2:T(8,128)(2,1)}) %reduce-scatter.3.cloned.1.call-update) | async-done | bytes 24592 | tf_op jit(solution)/shard_map/reduce_scatter | solution.py:43
  47.9 1.4 %multiply_convert_fusion = (bf16[8,1,1,1536]{3,0,1,2:T(8,128)(2,1)S(1)}, bf16[8,1,1,1536]{3,0,2,1:T(8,128)(2,1)}) fusion(bf16[8,1,1,1536]{3,0,1,2:T(8,128)(2,1)} %reduce-scatter.3.cloned.1.call-done), kind=kLoop, calls=%fused_computation.19 | loop fusion | flops 36864 | bytes 73728 | tf_op jit(solution)/shard_map/convert_element_type | solution.py:49
  49.2 5.3 %all_gather.7 = bf16[8,1,4,1536]{3,0,1,2:T(8,128)(2,1)S(1)} all-gather(bf16[8,1,1,1536]{3,0,1,2:T(8,128)(2,1)S(1)} %get-tuple-element.4), channel_id=1, replica_groups=mesh['rep'=2,'row'=4,'col'=4] {'row'}, dimensions={2}, use_global_device_ids=true | all-gather | bytes 122880 | tf_op jit(solution)/shard_map/all_gather | solution.py:50
  54.5 0.6 gather_fusion.1
  55.1 0.8 fusion.7
  55.9 0.0 copy-done.3
  55.9 0.5 convolution_bitcast_fusion
  56.3 0.1 reshape.98
  56.4 0.7 fusion.10
  57.1 0.0 reduce-scatter.5.cloned.1.call-update
  57.1 19.3 %reduce-scatter.5.cloned.1.call-done = bf16[8,1,1,1536]{3,0,1,2:T(8,128)(2,1)} async-done(((bf16[8,1,4,1536]{3,0,1,2:T(8,128)(2,1)}), bf16[8,1,1,1536]{3,0,1,2:T(8,128)(2,1)}) %reduce-scatter.5.cloned.1.call-update) | async-done | bytes 24592 | tf_op jit(solution)/shard_map/reduce_scatter | solution.py:53
  76.4 0.0 copy-done.1
  76.4 1.4 %fusion.16 = bf16[8,1,1,1536]{3,0,2,1:T(8,128)(2,1)} fusion(bf16[8,1,1,1536]{3,0,1,2:T(8,128)(2,1)} %reduce-scatter.5.cloned.1.call-done, bf16[8,1,1,1536]{3,0,2,1:T(8,128)(2,1)S(1)} %copy-done.1), kind=kLoop, calls=%fused_computation.20 | loop fusion | flops 61440 | bytes 73728
  (5 shorter events, 0.0 us)
Async XLA Ops:
  7.2 18.2 %copy-start = (bf16[1,1,8,384,384]{4,3,2,1,0:T(8,128)(2,1)S(1)}, bf16[1,1,8,384,384]{4,3,2,1,0:T(8,128)(2,1)}, u32[]{:S(2)}) copy-start(bf16[1,1,8,384,384]{4,3,2,1,0:T(8,128)(2,1)} %param.7) | copy-start | bytes 7077892
  7.2 18.7 %copy-start.2 = (s32[1,1,8]{2,1,0:T(1,128)S(1)}, s32[1,1,8]{2,1,0:T(1,128)}, u32[]{:S(2)}) copy-start(s32[1,1,8]{2,1,0:T(1,128)} %param.9) | copy-start | bytes 100
  7.2 40.7 %reduce-scatter.3.cloned.1.call-start = ((), (), s32[]{:S(2)}) async-start(), calls=%async_computation.2 | async-start | bytes 122880 | tf_op jit(solution)/shard_map/reduce_scatter | solution.py:43
  25.8 30.0 %copy-start.3 = (s32[1,1,8]{2,1,0:T(1,128)S(1)}, s32[1,1,8]{2,1,0:T(1,128)}, u32[]{:S(2)}) copy-start(s32[1,1,8]{2,1,0:T(1,128)} %param.8) | copy-start | bytes 100
  26.4 50.0 %copy-start.1 = (bf16[8,1,1,1536]{3,0,2,1:T(8,128)(2,1)S(1)}, bf16[8,1,1,1536]{3,0,2,1:T(8,128)(2,1)}, u32[]{:S(2)}) copy-start(bf16[8,1,1,1536]{3,0,2,1:T(8,128)(2,1)} %param.6) | copy-start | bytes 73732
  27.1 49.3 %reduce-scatter.5.cloned.1.call-start = ((), (), s32[]{:S(2)}) async-start(), calls=%async_computation.3 | async-start | bytes 122880 | tf_op jit(solution)/shard_map/reduce_scatter | solution.py:53
Sparse Core Ops, SparseCore 0:
  27.2 20.6 reduce-scatter.2
  57.3 19.0 reduce-scatter.4
where the time goes:
time: 84.9 us; the launch traced here: 84.6 us
  waiting for transfers between devices  40 us (47%)
  blocking collectives  20.6 us (24%)
  between operations  14.9 us (18%)
  other arithmetic  5.6 us (7%)
  matrix products  2.12 us (2%)
  local copies, waits for them, and re-layouts  1.31 us (2%)
    reduce_scatter x1, waiting for transfers between devices, on_device(): lax.psum_scatter(partial_value.reshape(vectors, 1, groups, piece_len).ast...  20.7 us
    reduce_scatter x1, waiting for transfers between devices, on_device(): lax.psum_scatter(second_partial.reshape(vectors, 1, groups, piece_len).as...  19.3 us
    all_gather x1, blocking collectives, on_device(): lax.all_gather(noise, 'col', axis=2, tiled=True).reshape(vectors, -1)  15.2 us
    all_gather x1, blocking collectives, on_device(): lax.all_gather(first_term, 'row', axis=2, tiled=True).reshape(vectors, -1)  5.32 us
  transfers between devices with their start and end apart: 2, of which 2 were waited for; matrix products, arithmetic and copies ran while one was open for 0% of the time, Pallas kernels for 0%

commit v1 on v0

v1 whole, which is shorter than its diff:
```python
import functools

import jax
import jax.numpy as jnp
from jax import lax
from jax.experimental import pallas as pl
from jax.experimental.pallas import tpu as pltpu
from jax.sharding import PartitionSpec as P

SHIFT = 1.0
HALF_WIDTH = 0.75

VMEM = pl.BlockSpec(memory_space=pltpu.VMEM)
SMEM = pl.BlockSpec(memory_space=pltpu.SMEM)


def pairing(size):
    if size & (size - 1) == 0:
        return (lambda i, k: i ^ k), (lambda i, k: i ^ k)
    return (lambda i, k: (i + k) % size), (lambda i, k: (i + size - k) % size)


def exchange(pieces, axis, size):
    to, _ = pairing(size)
    return [
        lax.ppermute(pieces[k - 1], axis, [(i, to(i, k)) for i in range(size)])
        for k in range(size - 1, 0, -1)
    ][::-1]


def lanes(start, length):
    return pl.ds(pl.multiple_of(start, 128), length)


def add_slots(source, total, tiles, read_at, write_at, live, contract):
    slots, span, _ = tiles.shape
    products = []
    for s in range(slots):
        picked = source[:, lanes(read_at[0, 0, s] * span, span)]
        products.append(
            lax.dot_general(
                picked, tiles[s], (((1,), (contract,)), ((), ())), preferred_element_type=jnp.float32
            )
        )
    for s in range(slots):
        at = lanes(write_at[0, 0, s] * span, span)
        total[:, at] += jnp.where(s < live, products[s], 0.0)


def self_factor():
    return (lax.axis_index("row") == lax.axis_index("col")).astype(jnp.float32)


def first_kernel(size, *refs):
    pieces, (tiles, rows, cols, count, self_mobility, out, whole, total) = refs[:size], refs[size:]
    _, source_of = pairing(size)
    me = lax.axis_index("col")
    piece = pieces[0].shape[1]
    for k in range(size):
        whole[:, lanes(source_of(me, k) * piece, piece)] = pieces[k][...]
    shift = self_factor() * (self_mobility[...] - SHIFT)
    total[...] = shift * whole[...].astype(jnp.float32)
    add_slots(whole, total, tiles, rows, cols, count[0, 0], 0)
    out[...] = total[...].astype(out.dtype)


def second_kernel(n_row, n_col, *refs):
    parts, (tiles, rows, cols, count, self_mobility), rest = (
        refs[:n_row],
        refs[n_row : n_row + 5],
        refs[n_row + 5 :],
    )
    first, outs, (whole, total) = rest[0], rest[1 : 1 + n_col], rest[1 + n_col :]
    sums = parts[0][...].astype(jnp.float32)
    for part in parts[1:]:
        sums = sums + part[...].astype(jnp.float32)
    whole[...] = (sums / HALF_WIDTH).astype(whole.dtype)
    row_piece = first.shape[1]
    first[...] = whole[:, lanes(lax.axis_index("row") * row_piece, row_piece)]
    shift = self_factor() * (self_mobility[...] - SHIFT)
    total[...] = shift * whole[...].astype(jnp.float32)
    add_slots(whole, total, tiles, cols, rows, count[0, 0], 1)
    to, _ = pairing(n_col)
    me = lax.axis_index("col")
    piece = outs[0].shape[1]
    for k in range(n_col):
        outs[k][...] = total[:, lanes(to(me, k) * piece, piece)].astype(outs[k].dtype)


def last_kernel(size, *refs):
    parts, (noise, out) = refs[:size], refs[size:]
    sums = parts[0][...].astype(jnp.float32)
    for part in parts[1:]:
        sums = sums + part[...].astype(jnp.float32)
    out[...] = (2.0 * sums / HALF_WIDTH - noise[...].astype(jnp.float32)).astype(out.dtype)


def on_device(noise, block_values, block_rows, block_cols, block_count, self_mobility):
    vectors, piece = noise.shape[0], noise.shape[3]
    n_row, n_col = lax.axis_size("row"), lax.axis_size("col")
    group_len = self_mobility.shape[1]
    own = noise.reshape(vectors, piece)
    tiles = block_values.reshape(block_values.shape[2:])
    whole_type = jax.ShapeDtypeStruct((vectors, group_len), jnp.bfloat16)
    piece_type = jax.ShapeDtypeStruct((vectors, piece), jnp.bfloat16)
    row_type = jax.ShapeDtypeStruct((vectors, group_len // n_row), jnp.bfloat16)
    table_specs = [VMEM, SMEM, SMEM, SMEM, VMEM]
    tables = (tiles, block_rows, block_cols, block_count, self_mobility)
    scratch = [
        pltpu.VMEM((vectors, group_len), jnp.bfloat16),
        pltpu.VMEM((vectors, group_len), jnp.float32),
    ]
    pieces = [own] + exchange([own] * (n_col - 1), "col", n_col)
    part = pl.pallas_call(
        functools.partial(first_kernel, n_col),
        out_shape=whole_type,
        in_specs=[VMEM] * n_col + table_specs,
        out_specs=VMEM,
        scratch_shapes=scratch,
        name="first_product",
    )(*pieces, *tables)
    parts = [part] + exchange([part] * (n_row - 1), "row", n_row)
    first, *seconds = pl.pallas_call(
        functools.partial(second_kernel, n_row, n_col),
        out_shape=[row_type] + [piece_type] * n_col,
        in_specs=[VMEM] * n_row + table_specs,
        out_specs=[VMEM] * (1 + n_col),
        scratch_shapes=scratch,
        name="second_product",
    )(*parts, *tables)
    arrived = [seconds[0]] + exchange(seconds[1:], "col", n_col)
    second = pl.pallas_call(
        functools.partial(last_kernel, n_col),
        out_shape=piece_type,
        in_specs=[VMEM] * (n_col + 1),
        out_specs=VMEM,
        name="second_term",
    )(*arrived, own)
    return first.reshape(vectors, 1, 1, -1), second.reshape(vectors, 1, 1, -1)


def solution(mesh):
    placed = (
        P("rep", "row", "col", None),
        P(("rep", "row"), "col", None, None, None),
        P(("rep", "row"), "col", None),
        P(("rep", "row"), "col", None),
        P(("rep", "row"), "col"),
        P(("rep", "row"), None),
    )
    return jax.shard_map(
        on_device,
        mesh=mesh,
        in_specs=placed,
        out_specs=(P("rep", "col", "row", None), P("rep", "row", "col", None)),
        check_vma=False,
    )
```

time: 84.9 us -> 36.5 us (0.43)
  waiting for transfers between devices: 40 us -> 12.7 us
  blocking collectives: 20.6 us -> 0 us
  between operations: 14.9 us -> 1.31 us
  starting transfers between devices: 0.08 us -> 12 us
  Pallas kernels: 0 us -> 7.71 us
  other arithmetic: 5.6 us -> 0 us
  matrix products: 2.12 us -> 0 us
  local copies, waits for them, and re-layouts: 1.31 us -> 2.5 us
    reduce_scatter x2 -> x0, waiting for transfers between devices: 40 us -> none  [the longest x1 20.7 us: on_device(): lax.psum_scatter(partial_value.reshape(vectors, 1, groups, piece_len).ast...]
    all_gather x2 -> x0, blocking collectives: 20.6 us -> none  [the longest x1 15.2 us: on_device(): lax.all_gather(noise, 'col', axis=2, tiled=True).reshape(vectors, -1)]
    ppermute x0 -> x9, waiting for transfers between devices: none -> 12.7 us  [exchange(): lax.ppermute(pieces[k - 1], axis, [(i, to(i, k)) for i in range(size)])]
    ppermute x0 -> x9, starting transfers between devices: none -> 12 us  [exchange(): lax.ppermute(pieces[k - 1], axis, [(i, to(i, k)) for i in range(size)])]
    pallas_call x0 -> x3, Pallas kernels: none -> 7.71 us  [the longest x1 3.38 us: on_device(): pl.pallas_call(functools.partial(second_kernel, n_row, n_col), out_shape=...]
    convert_element_type x4 -> x0, other arithmetic: 2.76 us -> none  [the longest x1 1.35 us: on_device(): first_term = (shares / HALF_WIDTH).astype(jnp.bfloat16)]
    unnamed x8 -> x18, local copies, waits for them, and re-layouts: 0.02 us -> 2.5 us
    dot_general x4 -> x0, matrix products: 2.12 us -> none  [the longest x2 0.9 us: slot_products(): jnp.einsum('vsm,sg->vgm', product, placing, precision=lax.Precision.HIGHEST)]
  transfers between devices with their start and end apart: 2 -> 9, of which waited for: 2 -> 6; matrix products, arithmetic and copies ran while one was open for 0% -> 0% of each run, Pallas kernels for 0% -> 0%
where the time goes in v1:
time: 36.5 us; the launch traced here: 36.2 us
  waiting for transfers between devices  12.7 us (35%)
  starting transfers between devices  12 us (33%)
  Pallas kernels  7.71 us (21%)
  local copies, waits for them, and re-layouts  2.5 us (7%)
  between operations  1.31 us (4%)
    ppermute x9, waiting for transfers between devices, exchange(): lax.ppermute(pieces[k - 1], axis, [(i, to(i, k)) for i in range(size)])  12.7 us
    ppermute x9, starting transfers between devices, exchange(): lax.ppermute(pieces[k - 1], axis, [(i, to(i, k)) for i in range(size)])  12 us
    pallas_call x1, Pallas kernels, on_device(): pl.pallas_call(functools.partial(second_kernel, n_row, n_col), out_shape=...  3.38 us
    pallas_call x1, Pallas kernels, on_device(): pl.pallas_call(functools.partial(first_kernel, n_col), out_shape=whole_ty...  2.89 us
    unnamed x18, local copies, waits for them, and re-layouts  2.5 us
    pallas_call x1, Pallas kernels, on_device(): pl.pallas_call(functools.partial(last_kernel, n_col), out_shape=piece_typ...  1.44 us
  transfers between devices with their start and end apart: 9, of which 6 were waited for; matrix products, arithmetic and copies ran while one was open for 0% of the time, Pallas kernels for 0%

profile of v1, /device:TPU:0, one launch (start us, length us, event | category | flops | bytes accessed | tf_op | source)
XLA Modules:
  0.0 36.2 jit_solution(1523790522800447517)
XLA Ops:
  0.6 5.1 %collective-permute-start.2 = (bf16[8,1536]{1,0:T(8,128)(2,1)}, bf16[8,1536]{1,0:T(8,128)(2,1)S(1)}, u32[]{:S(2)}, u32[]{:S(2)}) collective-permute-start(bf16[8,1536]{1,0:T(8,128)(2,1)} %bitcast.6), channel_id=1, source_target_pairs={{0,3},{1,2},{2,1},{3,0},{4,7},{5,6},{6,5},{7,4},{8,11},{9,10},{10,... | collective-permute-start | bytes 73736 | tf_op jit(solution)/shard_map/ppermute | solution.py:26
  5.7 0.0 collective-permute-start.1
  5.7 0.6 %collective-permute-start = (bf16[8,1536]{1,0:T(8,128)(2,1)}, bf16[8,1536]{1,0:T(8,128)(2,1)S(1)}, u32[]{:S(2)}, u32[]{:S(2)}) collective-permute-start(bf16[8,1536]{1,0:T(8,128)(2,1)} %bitcast.8), channel_id=1, source_target_pairs={{0,1},{1,0},{2,3},{3,2},{4,5},{5,4},{6,7},{7,6},{8,9},{9,8},{10,11... | collective-permute-start | bytes 73736 | tf_op jit(solution)/shard_map/ppermute | solution.py:26
  7.0 0.7 %collective-permute-done.2.refs_3_ = bf16[8,1536]{1,0:T(8,128)(2,1)S(1)} collective-permute-done((bf16[8,1536]{1,0:T(8,128)(2,1)}, bf16[8,1536]{1,0:T(8,128)(2,1)S(1)}, u32[]{:S(2)}, u32[]{:S(2)}) %collective-permute-start.2) | collective-permute-done | bytes 24608 | tf_op jit(solution)/shard_map/ppermute | solution.py:26
  7.8 0.0 copy-start.3
  7.8 2.9 %collective-permute-done.1.refs_2_ = bf16[8,1536]{1,0:T(8,128)(2,1)S(1)} collective-permute-done((bf16[8,1536]{1,0:T(8,128)(2,1)}, bf16[8,1536]{1,0:T(8,128)(2,1)S(1)}, u32[]{:S(2)}, u32[]{:S(2)}) %collective-permute-start.1) | collective-permute-done | bytes 24608 | tf_op jit(solution)/shard_map/ppermute | solution.py:26
  10.7 0.0 copy-start.4
  10.7 0.0 collective-permute-done.refs_1_
  10.7 0.0 copy-start.5
  10.7 0.0 copy-done.3
  10.7 0.6 %copy-done.4 = bf16[8,1536]{1,0:T(8,128)(2,1)} copy-done((bf16[8,1536]{1,0:T(8,128)(2,1)}, bf16[8,1536]{1,0:T(8,128)(2,1)S(1)}, u32[]{:S(2)}) %copy-start.4) | copy-done | bytes 24600
  11.3 0.0 copy-done.5
  11.3 2.9 %first_product.1.refs_0_ = bf16[8,6144]{1,0:T(8,128)(2,1)} custom-call(bf16[8,1536]{1,0:T(8,128)(2,1)} %bitcast.9, bf16[8,1536]{1,0:T(8,128)(2,1)} %copy-done.5, bf16[8,1536]{1,0:T(8,128)(2,1)} %copy-done.4, bf16[8,1536]{1,0:T(8,128)(2,1)} %copy-done.3, bf16[8,384,384]{2,1,0:T(8,128)(2,1)} %bitcast.4, s32[1,1,8]{2,1,0:T(1,128)} %refs_5_.3, ...), custom_call_target="tpu_custom_call" | custom-call | tf_op jit(solution)/shard_map/first_product/pallas_call | solution.py:114
  14.2 0.0 collective-permute-start.5
  14.2 1.5 %collective-permute-start.4 = (bf16[8,6144]{1,0:T(8,128)(2,1)}, bf16[8,6144]{1,0:T(8,128)(2,1)S(1)}, u32[]{:S(2)}, u32[]{:S(2)}) collective-permute-start(bf16[8,6144]{1,0:T(8,128)(2,1)} %first_product.1.refs_0_), channel_id=1, source_target_pairs={{0,8},{4,12},{8,0},{12,4},{1,9},{5,13},{9,1},{13,5},{2,10},{6,14},... | collective-permute-start | bytes 294920 | tf_op jit(solution)/shard_map/ppermute | solution.py:26
  15.7 0.3 collective-permute-start.3
  16.1 3.4 %collective-permute-done.5.refs_3_ = bf16[8,6144]{1,0:T(8,128)(2,1)S(1)} collective-permute-done((bf16[8,6144]{1,0:T(8,128)(2,1)}, bf16[8,6144]{1,0:T(8,128)(2,1)S(1)}, u32[]{:S(2)}, u32[]{:S(2)}) %collective-permute-start.5) | collective-permute-done | bytes 98336 | tf_op jit(solution)/shard_map/ppermute | solution.py:26
  19.4 0.0 copy-start
  19.4 2.2 %collective-permute-done.4.refs_2_ = bf16[8,6144]{1,0:T(8,128)(2,1)S(1)} collective-permute-done((bf16[8,6144]{1,0:T(8,128)(2,1)}, bf16[8,6144]{1,0:T(8,128)(2,1)S(1)}, u32[]{:S(2)}, u32[]{:S(2)}) %collective-permute-start.4) | collective-permute-done | bytes 98336 | tf_op jit(solution)/shard_map/ppermute | solution.py:26
  21.6 0.0 copy-start.1
  21.6 0.0 collective-permute-done.3.refs_1_
  21.6 0.0 copy-done
  21.6 0.6 %copy-done.1 = bf16[8,6144]{1,0:T(8,128)(2,1)} copy-done((bf16[8,6144]{1,0:T(8,128)(2,1)}, bf16[8,6144]{1,0:T(8,128)(2,1)S(1)}, u32[]{:S(2)}) %copy-start.1) | copy-done | bytes 98328
  22.3 0.0 copy-start.2
  22.3 0.6 %copy-done.2 = bf16[8,6144]{1,0:T(8,128)(2,1)} copy-done((bf16[8,6144]{1,0:T(8,128)(2,1)}, bf16[8,6144]{1,0:T(8,128)(2,1)S(1)}, u32[]{:S(2)}) %copy-start.2) | copy-done | bytes 98328
  22.9 3.4 %second_product.1 = (bf16[8,1536]{1,0:T(8,128)(2,1)}, bf16[8,1536]{1,0:T(8,128)(2,1)}, bf16[8,1536]{1,0:T(8,128)(2,1)}, bf16[8,1536]{1,0:T(8,128)(2,1)}, bf16[8,1536]{1,0:T(8,128)(2,1)}) custom-call(bf16[8,6144]{1,0:T(8,128)(2,1)} %first_product.1.refs_0_, bf16[8,6144]{1,0:T(8,128)(2,1)} %copy-done.2, bf16[8,6144]{1,0:T(8,128)(2,1)} %copy-done.1, ...), custom_call_target="tpu_custom_call" | custom-call | tf_op jit(solution)/shard_map/second_product/pallas_call | solution.py:123
  26.3 0.0 collective-permute-start.6
  26.3 2.1 %collective-permute-start.7 = (bf16[8,1536]{1,0:T(8,128)(2,1)}, bf16[8,1536]{1,0:T(8,128)(2,1)S(1)}, u32[]{:S(2)}, u32[]{:S(2)}) collective-permute-start(bf16[8,1536]{1,0:T(8,128)(2,1)} %get-tuple-element.10), channel_id=1, source_target_pairs={{0,2},{1,3},{2,0},{3,1},{4,6},{5,7},{6,4},{7,5},{8,10},{9,11},{10,... | collective-permute-start | bytes 73736 | tf_op jit(solution)/shard_map/ppermute | solution.py:26
  28.4 2.3 %collective-permute-start.8 = (bf16[8,1536]{1,0:T(8,128)(2,1)}, bf16[8,1536]{1,0:T(8,128)(2,1)S(1)}, u32[]{:S(2)}, u32[]{:S(2)}) collective-permute-start(bf16[8,1536]{1,0:T(8,128)(2,1)} %get-tuple-element.11), channel_id=1, source_target_pairs={{0,3},{1,2},{2,1},{3,0},{4,7},{5,6},{6,5},{7,4},{8,11},{9,10},{10,... | collective-permute-start | bytes 73736 | tf_op jit(solution)/shard_map/ppermute | solution.py:26
  30.7 0.0 collective-permute-done.6.refs_1_
  30.7 0.0 copy-start.6
  30.7 0.6 %collective-permute-done.7.refs_2_ = bf16[8,1536]{1,0:T(8,128)(2,1)S(1)} collective-permute-done((bf16[8,1536]{1,0:T(8,128)(2,1)}, bf16[8,1536]{1,0:T(8,128)(2,1)S(1)}, u32[]{:S(2)}, u32[]{:S(2)}) %collective-permute-start.7) | collective-permute-done | bytes 24608 | tf_op jit(solution)/shard_map/ppermute | solution.py:26
  31.3 0.0 copy-start.7
  31.3 2.9 %collective-permute-done.8.refs_3_ = bf16[8,1536]{1,0:T(8,128)(2,1)S(1)} collective-permute-done((bf16[8,1536]{1,0:T(8,128)(2,1)}, bf16[8,1536]{1,0:T(8,128)(2,1)S(1)}, u32[]{:S(2)}, u32[]{:S(2)}) %collective-permute-start.8) | collective-permute-done | bytes 24608 | tf_op jit(solution)/shard_map/ppermute | solution.py:26
  34.2 0.0 copy-start.8
  34.2 0.0 copy-done.6
  34.2 0.0 copy-done.7
  34.2 0.6 %copy-done.8 = bf16[8,1536]{1,0:T(8,128)(2,1)} copy-done((bf16[8,1536]{1,0:T(8,128)(2,1)}, bf16[8,1536]{1,0:T(8,128)(2,1)S(1)}, u32[]{:S(2)}) %copy-start.8) | copy-done | bytes 24600
  34.8 1.4 %second_term.1 = bf16[8,1536]{1,0:T(8,128)(2,1)} custom-call(bf16[8,1536]{1,0:T(8,128)(2,1)} %get-tuple-element.8.refs_0_, bf16[8,1536]{1,0:T(8,128)(2,1)} %copy-done.6, bf16[8,1536]{1,0:T(8,128)(2,1)} %copy-done.7, bf16[8,1536]{1,0:T(8,128)(2,1)} %copy-done.8, bf16[8,1536]{1,0:T(8,128)(2,1)} %bitcast.10), custom_call_target="tpu_custom_call" | custom-call | tf_op jit(solution)/shard_map/second_term/pallas_call | solution.py:132
Async XLA Ops:
  0.6 7.1 %collective-permute-start.2 = (bf16[8,1536]{1,0:T(8,128)(2,1)}, bf16[8,1536]{1,0:T(8,128)(2,1)S(1)}, u32[]{:S(2)}, u32[]{:S(2)}) collective-permute-start(bf16[8,1536]{1,0:T(8,128)(2,1)} %bitcast.6), channel_id=1, source_target_pairs={{0,3},{1,2},{2,1},{3,0},{4,7},{5,6},{6,5},{7,4},{8,11},{9,10},{10,... | collective-permute-start | bytes 73736 | tf_op jit(solution)/shard_map/ppermute | solution.py:26
  5.7 4.9 %collective-permute-start.1 = (bf16[8,1536]{1,0:T(8,128)(2,1)}, bf16[8,1536]{1,0:T(8,128)(2,1)S(1)}, u32[]{:S(2)}, u32[]{:S(2)}) collective-permute-start(bf16[8,1536]{1,0:T(8,128)(2,1)} %bitcast.7), channel_id=1, source_target_pairs={{0,2},{1,3},{2,0},{3,1},{4,6},{5,7},{6,4},{7,5},{8,10},{9,11},{10,... | collective-permute-start | bytes 73736 | tf_op jit(solution)/shard_map/ppermute | solution.py:26
  5.7 4.9 %collective-permute-start = (bf16[8,1536]{1,0:T(8,128)(2,1)}, bf16[8,1536]{1,0:T(8,128)(2,1)S(1)}, u32[]{:S(2)}, u32[]{:S(2)}) collective-permute-start(bf16[8,1536]{1,0:T(8,128)(2,1)} %bitcast.8), channel_id=1, source_target_pairs={{0,1},{1,0},{2,3},{3,2},{4,5},{5,4},{6,7},{7,6},{8,9},{9,8},{10,11... | collective-permute-start | bytes 73736 | tf_op jit(solution)/shard_map/ppermute | solution.py:26
  7.8 2.9 %copy-start.3 = (bf16[8,1536]{1,0:T(8,128)(2,1)}, bf16[8,1536]{1,0:T(8,128)(2,1)S(1)}, u32[]{:S(2)}) copy-start(bf16[8,1536]{1,0:T(8,128)(2,1)S(1)} %collective-permute-done.2.refs_3_) | copy-start | bytes 73732
  10.7 0.6 %copy-start.4 = (bf16[8,1536]{1,0:T(8,128)(2,1)}, bf16[8,1536]{1,0:T(8,128)(2,1)S(1)}, u32[]{:S(2)}) copy-start(bf16[8,1536]{1,0:T(8,128)(2,1)S(1)} %collective-permute-done.1.refs_2_) | copy-start | bytes 73732
  10.7 0.6 %copy-start.5 = (bf16[8,1536]{1,0:T(8,128)(2,1)}, bf16[8,1536]{1,0:T(8,128)(2,1)S(1)}, u32[]{:S(2)}) copy-start(bf16[8,1536]{1,0:T(8,128)(2,1)S(1)} %collective-permute-done.refs_1_) | copy-start | bytes 73732
  14.2 5.3 %collective-permute-start.5 = (bf16[8,6144]{1,0:T(8,128)(2,1)}, bf16[8,6144]{1,0:T(8,128)(2,1)S(1)}, u32[]{:S(2)}, u32[]{:S(2)}) collective-permute-start(bf16[8,6144]{1,0:T(8,128)(2,1)} %first_product.1.refs_0_), channel_id=1, source_target_pairs={{0,12},{4,8},{8,4},{12,0},{1,13},{5,9},{9,5},{13,1},{2,14},{6,10},... | collective-permute-start | bytes 294920 | tf_op jit(solution)/shard_map/ppermute | solution.py:26
  14.2 7.4 %collective-permute-start.4 = (bf16[8,6144]{1,0:T(8,128)(2,1)}, bf16[8,6144]{1,0:T(8,128)(2,1)S(1)}, u32[]{:S(2)}, u32[]{:S(2)}) collective-permute-start(bf16[8,6144]{1,0:T(8,128)(2,1)} %first_product.1.refs_0_), channel_id=1, source_target_pairs={{0,8},{4,12},{8,0},{12,4},{1,9},{5,13},{9,1},{13,5},{2,10},{6,14},... | collective-permute-start | bytes 294920 | tf_op jit(solution)/shard_map/ppermute | solution.py:26
  15.7 5.9 %collective-permute-start.3 = (bf16[8,6144]{1,0:T(8,128)(2,1)}, bf16[8,6144]{1,0:T(8,128)(2,1)S(1)}, u32[]{:S(2)}, u32[]{:S(2)}) collective-permute-start(bf16[8,6144]{1,0:T(8,128)(2,1)} %first_product.1.refs_0_), channel_id=1, source_target_pairs={{0,4},{4,0},{8,12},{12,8},{1,5},{5,1},{9,13},{13,9},{2,6},{6,2},{1... | collective-permute-start | bytes 294920 | tf_op jit(solution)/shard_map/ppermute | solution.py:26
  19.4 2.2 %copy-start = (bf16[8,6144]{1,0:T(8,128)(2,1)}, bf16[8,6144]{1,0:T(8,128)(2,1)S(1)}, u32[]{:S(2)}) copy-start(bf16[8,6144]{1,0:T(8,128)(2,1)S(1)} %collective-permute-done.5.refs_3_) | copy-start | bytes 294916
  21.6 0.6 %copy-start.1 = (bf16[8,6144]{1,0:T(8,128)(2,1)}, bf16[8,6144]{1,0:T(8,128)(2,1)S(1)}, u32[]{:S(2)}) copy-start(bf16[8,6144]{1,0:T(8,128)(2,1)S(1)} %collective-permute-done.4.refs_2_) | copy-start | bytes 294916
  22.3 0.6 %copy-start.2 = (bf16[8,6144]{1,0:T(8,128)(2,1)}, bf16[8,6144]{1,0:T(8,128)(2,1)S(1)}, u32[]{:S(2)}) copy-start(bf16[8,6144]{1,0:T(8,128)(2,1)S(1)} %collective-permute-done.3.refs_1_) | copy-start | bytes 294916
  26.3 4.4 %collective-permute-start.6 = (bf16[8,1536]{1,0:T(8,128)(2,1)}, bf16[8,1536]{1,0:T(8,128)(2,1)S(1)}, u32[]{:S(2)}, u32[]{:S(2)}) collective-permute-start(bf16[8,1536]{1,0:T(8,128)(2,1)} %get-tuple-element.9), channel_id=1, source_target_pairs={{0,1},{1,0},{2,3},{3,2},{4,5},{5,4},{6,7},{7,6},{8,9},{9,8},{10,11... | collective-permute-start | bytes 73736 | tf_op jit(solution)/shard_map/ppermute | solution.py:26
  26.3 5.0 %collective-permute-start.7 = (bf16[8,1536]{1,0:T(8,128)(2,1)}, bf16[8,1536]{1,0:T(8,128)(2,1)S(1)}, u32[]{:S(2)}, u32[]{:S(2)}) collective-permute-start(bf16[8,1536]{1,0:T(8,128)(2,1)} %get-tuple-element.10), channel_id=1, source_target_pairs={{0,2},{1,3},{2,0},{3,1},{4,6},{5,7},{6,4},{7,5},{8,10},{9,11},{10,... | collective-permute-start | bytes 73736 | tf_op jit(solution)/shard_map/ppermute | solution.py:26
  28.4 5.8 %collective-permute-start.8 = (bf16[8,1536]{1,0:T(8,128)(2,1)}, bf16[8,1536]{1,0:T(8,128)(2,1)S(1)}, u32[]{:S(2)}, u32[]{:S(2)}) collective-permute-start(bf16[8,1536]{1,0:T(8,128)(2,1)} %get-tuple-element.11), channel_id=1, source_target_pairs={{0,3},{1,2},{2,1},{3,0},{4,7},{5,6},{6,5},{7,4},{8,11},{9,10},{10,... | collective-permute-start | bytes 73736 | tf_op jit(solution)/shard_map/ppermute | solution.py:26
  30.7 3.5 %copy-start.6 = (bf16[8,1536]{1,0:T(8,128)(2,1)}, bf16[8,1536]{1,0:T(8,128)(2,1)S(1)}, u32[]{:S(2)}) copy-start(bf16[8,1536]{1,0:T(8,128)(2,1)S(1)} %collective-permute-done.6.refs_1_) | copy-start | bytes 73732
  31.3 2.9 %copy-start.7 = (bf16[8,1536]{1,0:T(8,128)(2,1)}, bf16[8,1536]{1,0:T(8,128)(2,1)S(1)}, u32[]{:S(2)}) copy-start(bf16[8,1536]{1,0:T(8,128)(2,1)S(1)} %collective-permute-done.7.refs_2_) | copy-start | bytes 73732
  34.2 0.6 %copy-start.8 = (bf16[8,1536]{1,0:T(8,128)(2,1)}, bf16[8,1536]{1,0:T(8,128)(2,1)S(1)}, u32[]{:S(2)}) copy-start(bf16[8,1536]{1,0:T(8,128)(2,1)S(1)} %collective-permute-done.8.refs_3_) | copy-start | bytes 73732

commit v2 on v1

--- a/solution.py
+++ b/solution.py
@@ -9,8 +9,11 @@
 
 SHIFT = 1.0
 HALF_WIDTH = 0.75
+VMEM_LIMIT = 8 << 20
+STAGE_LIMIT = 50 << 20
 
 VMEM = pl.BlockSpec(memory_space=pltpu.VMEM)
+HBM = pl.BlockSpec(memory_space=pltpu.HBM)
 SMEM = pl.BlockSpec(memory_space=pltpu.SMEM)
 
 
@@ -32,8 +35,9 @@
     return pl.ds(pl.multiple_of(start, 128), length)
 
 
-def add_slots(source, total, tiles, read_at, write_at, live, contract):
+def add_slots(source, total, tiles, read_at, write_at, count, contract):
     slots, span, _ = tiles.shape
+    live, spare = count[0, 0], source.shape[1] // span
     products = []
     for s in range(slots):
         picked = source[:, lanes(read_at[0, 0, s] * span, span)]
@@ -43,43 +47,45 @@
             )
         )
     for s in range(slots):
-        at = lanes(write_at[0, 0, s] * span, span)
-        total[:, at] += jnp.where(s < live, products[s], 0.0)
+        at = lanes(jnp.where(s < live, write_at[0, 0, s], spare) * span, span)
+        total[:, at] += products[s]
 
 
 def self_factor():
     return (lax.axis_index("row") == lax.axis_index("col")).astype(jnp.float32)
 
 
+def stage_kernel(values, tiles, sem):
+    copy = pltpu.make_async_copy(values, tiles, sem)
+    copy.start()
+    copy.wait()
+
+
 def first_kernel(size, *refs):
-    pieces, (tiles, rows, cols, count, self_mobility, out, whole, total) = refs[:size], refs[size:]
+    pieces, (tiles, rows, cols, count, mobility, out, whole, total) = refs[:size], refs[size:]
     _, source_of = pairing(size)
     me = lax.axis_index("col")
-    piece = pieces[0].shape[1]
+    piece, group_len = pieces[0].shape[1], whole.shape[1]
     for k in range(size):
         whole[:, lanes(source_of(me, k) * piece, piece)] = pieces[k][...]
-    shift = self_factor() * (self_mobility[...] - SHIFT)
-    total[...] = shift * whole[...].astype(jnp.float32)
-    add_slots(whole, total, tiles, rows, cols, count[0, 0], 0)
-    out[...] = total[...].astype(out.dtype)
+    total[:, :group_len] = self_factor() * (mobility[...] - SHIFT) * whole[...].astype(jnp.float32)
+    add_slots(whole, total, tiles, rows, cols, count, 0)
+    out[...] = total[:, :group_len].astype(out.dtype)
 
 
 def second_kernel(n_row, n_col, *refs):
-    parts, (tiles, rows, cols, count, self_mobility), rest = (
-        refs[:n_row],
-        refs[n_row : n_row + 5],
-        refs[n_row + 5 :],
-    )
+    parts, rest = refs[:n_row], refs[n_row + 5 :]
+    tiles, rows, cols, count, mobility = refs[n_row : n_row + 5]
     first, outs, (whole, total) = rest[0], rest[1 : 1 + n_col], rest[1 + n_col :]
+    group_len = whole.shape[1]
     sums = parts[0][...].astype(jnp.float32)
     for part in parts[1:]:
         sums = sums + part[...].astype(jnp.float32)
-    whole[...] = (sums / HALF_WIDTH).astype(whole.dtype)
+    whole[...] = (sums * (1.0 / HALF_WIDTH)).astype(whole.dtype)
     row_piece = first.shape[1]
     first[...] = whole[:, lanes(lax.axis_index("row") * row_piece, row_piece)]
-    shift = self_factor() * (self_mobility[...] - SHIFT)
-    total[...] = shift * whole[...].astype(jnp.float32)
-    add_slots(whole, total, tiles, cols, rows, count[0, 0], 1)
+    total[:, :group_len] = self_factor() * (mobility[...] - SHIFT) * whole[...].astype(jnp.float32)
+    add_slots(whole, total, tiles, cols, rows, count, 1)
     to, _ = pairing(n_col)
     me = lax.axis_index("col")
     piece = outs[0].shape[1]
@@ -92,7 +98,7 @@
     sums = parts[0][...].astype(jnp.float32)
     for part in parts[1:]:
         sums = sums + part[...].astype(jnp.float32)
-    out[...] = (2.0 * sums / HALF_WIDTH - noise[...].astype(jnp.float32)).astype(out.dtype)
+    out[...] = ((2.0 / HALF_WIDTH) * sums - noise[...].astype(jnp.float32)).astype(out.dtype)
 
 
 def on_device(noise, block_values, block_rows, block_cols, block_count, self_mobility):
@@ -104,19 +110,33 @@
     whole_type = jax.ShapeDtypeStruct((vectors, group_len), jnp.bfloat16)
     piece_type = jax.ShapeDtypeStruct((vectors, piece), jnp.bfloat16)
     row_type = jax.ShapeDtypeStruct((vectors, group_len // n_row), jnp.bfloat16)
-    table_specs = [VMEM, SMEM, SMEM, SMEM, VMEM]
-    tables = (tiles, block_rows, block_cols, block_count, self_mobility)
+    span, slots = tiles.shape[-1], tiles.shape[0]
     scratch = [
         pltpu.VMEM((vectors, group_len), jnp.bfloat16),
-        pltpu.VMEM((vectors, group_len), jnp.float32),
+        pltpu.VMEM((vectors, group_len + span), jnp.float32),
     ]
-    pieces = [own] + exchange([own] * (n_col - 1), "col", n_col)
+    params = pltpu.CompilerParams(vmem_limit_bytes=VMEM_LIMIT)
+    arrived = exchange([own] * (n_col - 1), "col", n_col)
+    staged = pl.pallas_call(
+        stage_kernel,
+        out_shape=jax.ShapeDtypeStruct(tiles.shape, tiles.dtype),
+        in_specs=[HBM],
+        out_specs=VMEM,
+        scratch_shapes=[pltpu.SemaphoreType.DMA],
+        compiler_params=pltpu.CompilerParams(vmem_limit_bytes=STAGE_LIMIT),
+        cost_estimate=pl.CostEstimate(flops=0, transcendentals=0, bytes_accessed=4 * tiles.size),
+        name="stage",
+    )(tiles)
+    tables = (staged, block_rows, block_cols, block_count, self_mobility)
+    table_specs = [VMEM, SMEM, SMEM, SMEM, VMEM]
+    pieces = [own] + arrived
     part = pl.pallas_call(
         functools.partial(first_kernel, n_col),
         out_shape=whole_type,
         in_specs=[VMEM] * n_col + table_specs,
         out_specs=VMEM,
         scratch_shapes=scratch,
+        compiler_params=params,
         name="first_product",
     )(*pieces, *tables)
     parts = [part] + exchange([part] * (n_row - 1), "row", n_row)
@@ -126,6 +146,7 @@
         in_specs=[VMEM] * n_row + table_specs,
         out_specs=[VMEM] * (1 + n_col),
         scratch_shapes=scratch,
+        compiler_params=params,
         name="second_product",
     )(*parts, *tables)
     arrived = [seconds[0]] + exchange(seconds[1:], "col", n_col)
@@ -134,6 +155,7 @@
         out_shape=piece_type,
         in_specs=[VMEM] * (n_col + 1),
         out_specs=VMEM,
+        compiler_params=params,
         name="second_term",
     )(*arrived, own)
     return first.reshape(vectors, 1, 1, -1), second.reshape(vectors, 1, 1, -1)

time: 36.5 us -> 29.8 us (0.82)
  local copies, waits for them, and re-layouts: 2.5 us -> 0.02 us
  Pallas kernels: 7.71 us -> 5.24 us
  waiting for transfers between devices: 12.7 us -> 10.9 us
    unnamed x18 -> x8, local copies, waits for them, and re-layouts: 2.5 us -> 0.02 us
    pallas_call x1, Pallas kernels: 2.89 us -> 1.02 us  [on_device(): pl.pallas_call(functools.partial(first_kernel, n_col), out_shape=whole_ty...]
    ppermute x9, waiting for transfers between devices: 12.7 us -> 10.9 us  [exchange(): lax.ppermute(pieces[k - 1], axis, [(i, to(i, k)) for i in range(size)])]
    pallas_call x0 -> x1, Pallas kernels: none -> 1.7 us  [on_device(): pl.pallas_call(stage_kernel, out_shape=jax.ShapeDtypeStruct(tiles.shape,...]
    pallas_call x1, Pallas kernels: 3.38 us -> 1.89 us  [on_device(): pl.pallas_call(functools.partial(second_kernel, n_row, n_col), out_shape=...]
    pallas_call x1, Pallas kernels: 1.44 us -> 0.63 us  [on_device(): pl.pallas_call(functools.partial(last_kernel, n_col), out_shape=piece_typ...]
  transfers between devices with their start and end apart: 9 -> 9, of which waited for: 6 -> 5; matrix products, arithmetic and copies ran while one was open for 0% -> 0% of each run, Pallas kernels for 0% -> 6%
where the time goes in v2:
time: 29.8 us; the launch traced here: 29.6 us
  starting transfers between devices  12.1 us (41%)
  waiting for transfers between devices  10.9 us (37%)
  Pallas kernels  5.24 us (18%)
  between operations  1.37 us (5%)
    ppermute x9, starting transfers between devices, exchange(): lax.ppermute(pieces[k - 1], axis, [(i, to(i, k)) for i in range(size)])  12.1 us
    ppermute x9, waiting for transfers between devices, exchange(): lax.ppermute(pieces[k - 1], axis, [(i, to(i, k)) for i in range(size)])  10.9 us
    pallas_call x1, Pallas kernels, on_device(): pl.pallas_call(functools.partial(second_kernel, n_row, n_col), out_shape=...  1.89 us
    pallas_call x1, Pallas kernels, on_device(): pl.pallas_call(stage_kernel, out_shape=jax.ShapeDtypeStruct(tiles.shape,...  1.7 us
    pallas_call x1, Pallas kernels, on_device(): pl.pallas_call(functools.partial(first_kernel, n_col), out_shape=whole_ty...  1.02 us
    pallas_call x1, Pallas kernels, on_device(): pl.pallas_call(functools.partial(last_kernel, n_col), out_shape=piece_typ...  0.63 us
  transfers between devices with their start and end apart: 9, of which 5 were waited for; matrix products, arithmetic and copies ran while one was open for 0% of the time, Pallas kernels for 6%

profile of v2, /device:TPU:0, one launch (start us, length us, event | category | flops | bytes accessed | tf_op | source)
XLA Modules:
  0.0 29.6 jit_solution(4431429469371821346)
XLA Ops:
  0.6 5.1 %collective-permute-start.2 = (bf16[8,1536]{1,0:T(8,128)(2,1)}, bf16[8,1536]{1,0:T(8,128)(2,1)S(1)}, u32[]{:S(2)}, u32[]{:S(2)}) collective-permute-start(bf16[8,1536]{1,0:T(8,128)(2,1)} %bitcast.4), channel_id=1, source_target_pairs={{0,3},{1,2},{2,1},{3,0},{4,7},{5,6},{6,5},{7,4},{8,11},{9,10},{10,... | collective-permute-start | bytes 73736 | tf_op jit(solution)/shard_map/ppermute | solution.py:29
  5.7 0.0 collective-permute-start.1
  5.7 0.6 %collective-permute-start = (bf16[8,1536]{1,0:T(8,128)(2,1)}, bf16[8,1536]{1,0:T(8,128)(2,1)S(1)}, u32[]{:S(2)}, u32[]{:S(2)}) collective-permute-start(bf16[8,1536]{1,0:T(8,128)(2,1)} %bitcast.6), channel_id=1, source_target_pairs={{0,1},{1,0},{2,3},{3,2},{4,5},{5,4},{6,7},{7,6},{8,9},{9,8},{10,11... | collective-permute-start | bytes 73736 | tf_op jit(solution)/shard_map/ppermute | solution.py:29
  7.0 0.0 copy-start
  7.0 0.0 copy-start.1
  7.1 0.0 copy-start.2
  7.1 0.0 copy-start.3
  7.1 1.7 %stage.1.refs_4_ = bf16[8,384,384]{2,1,0:T(8,128)(2,1)S(1)} custom-call(bf16[8,384,384]{2,1,0:T(8,128)(2,1)} %bitcast.9), custom_call_target="tpu_custom_call" | custom-call | bytes 4718592 | tf_op jit(solution)/shard_map/stage/pallas_call | solution.py:120
  8.8 0.0 collective-permute-done.2.refs_3_
  8.8 1.9 %collective-permute-done.1.refs_2_ = bf16[8,1536]{1,0:T(8,128)(2,1)S(1)} collective-permute-done((bf16[8,1536]{1,0:T(8,128)(2,1)}, bf16[8,1536]{1,0:T(8,128)(2,1)S(1)}, u32[]{:S(2)}, u32[]{:S(2)}) %collective-permute-start.1) | collective-permute-done | bytes 24608 | tf_op jit(solution)/shard_map/ppermute | solution.py:29
  10.7 0.0 collective-permute-done.refs_1_
  10.7 0.0 copy-done
  10.7 0.0 copy-done.1
  10.7 0.0 copy-done.2
  10.7 0.0 copy-done.3
  10.7 1.0 %first_product.1.refs_0_ = bf16[8,6144]{1,0:T(8,128)(2,1)S(1)} custom-call(bf16[8,1536]{1,0:T(8,128)(2,1)S(1)} %bitcast.7, bf16[8,1536]{1,0:T(8,128)(2,1)S(1)} %collective-permute-done.refs_1_, bf16[8,1536]{1,0:T(8,128)(2,1)S(1)} %collective-permute-done.1.refs_2_, bf16[8,1536]{1,0:T(8,128)(2,1)S(1)} %collective-permute-done.2.refs_3_, ...), custom_call_target="tpu_custom_call" | custom-call | tf_op jit(solution)/shard_map/first_product/pallas_call | solution.py:133
  11.7 0.1 collective-permute-start.5
  11.8 1.6 %collective-permute-start.4 = (bf16[8,6144]{1,0:T(8,128)(2,1)S(1)}, bf16[8,6144]{1,0:T(8,128)(2,1)S(1)}, u32[]{:S(2)}, u32[]{:S(2)}) collective-permute-start(bf16[8,6144]{1,0:T(8,128)(2,1)S(1)} %first_product.1.refs_0_), channel_id=1, source_target_pairs={{0,8},{4,12},{8,0},{12,4},{1,9},{5,13},{9,1},{13,5},{2,10},{6,14},... | collective-permute-start | bytes 294920 | tf_op jit(solution)/shard_map/ppermute | solution.py:29
  13.4 0.3 collective-permute-start.3
  13.7 3.2 %collective-permute-done.5.refs_3_ = bf16[8,6144]{1,0:T(8,128)(2,1)S(1)} collective-permute-done((bf16[8,6144]{1,0:T(8,128)(2,1)S(1)}, bf16[8,6144]{1,0:T(8,128)(2,1)S(1)}, u32[]{:S(2)}, u32[]{:S(2)}) %collective-permute-start.5) | collective-permute-done | bytes 98336 | tf_op jit(solution)/shard_map/ppermute | solution.py:29
  16.9 2.2 %collective-permute-done.4.refs_2_ = bf16[8,6144]{1,0:T(8,128)(2,1)S(1)} collective-permute-done((bf16[8,6144]{1,0:T(8,128)(2,1)S(1)}, bf16[8,6144]{1,0:T(8,128)(2,1)S(1)}, u32[]{:S(2)}, u32[]{:S(2)}) %collective-permute-start.4) | collective-permute-done | bytes 98336 | tf_op jit(solution)/shard_map/ppermute | solution.py:29
  19.0 0.0 collective-permute-done.3.refs_1_
  19.0 1.9 %second_product.1 = (bf16[8,1536]{1,0:T(8,128)(2,1)}, bf16[8,1536]{1,0:T(8,128)(2,1)S(1)}, bf16[8,1536]{1,0:T(8,128)(2,1)S(1)}, bf16[8,1536]{1,0:T(8,128)(2,1)S(1)}, bf16[8,1536]{1,0:T(8,128)(2,1)S(1)}) custom-call(bf16[8,6144]{1,0:T(8,128)(2,1)S(1)} %first_product.1.refs_0_, bf16[8,6144]{1,0:T(8,128)(2,1)S(1)} %collective-permute-done.3.refs_1_, ...), custom_call_target="tpu_custom_call" | custom-call | tf_op jit(solution)/shard_map/second_product/pallas_call | solution.py:143
  20.9 0.0 collective-permute-start.6
  20.9 2.4 %collective-permute-start.7 = (bf16[8,1536]{1,0:T(8,128)(2,1)S(1)}, bf16[8,1536]{1,0:T(8,128)(2,1)S(1)}, u32[]{:S(2)}, u32[]{:S(2)}) collective-permute-start(bf16[8,1536]{1,0:T(8,128)(2,1)S(1)} %get-tuple-element.10), channel_id=1, source_target_pairs={{0,2},{1,3},{2,0},{3,1},{4,6},{5,7},{6,4},{7,5},{8,10},{9,11},{10,... | collective-permute-start | bytes 73736 | tf_op jit(solution)/shard_map/ppermute | solution.py:29
  23.4 1.9 %collective-permute-start.8 = (bf16[8,1536]{1,0:T(8,128)(2,1)S(1)}, bf16[8,1536]{1,0:T(8,128)(2,1)S(1)}, u32[]{:S(2)}, u32[]{:S(2)}) collective-permute-start(bf16[8,1536]{1,0:T(8,128)(2,1)S(1)} %get-tuple-element.11), channel_id=1, source_target_pairs={{0,3},{1,2},{2,1},{3,0},{4,7},{5,6},{6,5},{7,4},{8,11},{9,10},{10,... | collective-permute-start | bytes 73736 | tf_op jit(solution)/shard_map/ppermute | solution.py:29
  25.3 0.0 collective-permute-done.6.refs_1_
  25.3 0.3 %collective-permute-done.7.refs_2_ = bf16[8,1536]{1,0:T(8,128)(2,1)S(1)} collective-permute-done((bf16[8,1536]{1,0:T(8,128)(2,1)S(1)}, bf16[8,1536]{1,0:T(8,128)(2,1)S(1)}, u32[]{:S(2)}, u32[]{:S(2)}) %collective-permute-start.7) | collective-permute-done | bytes 24608 | tf_op jit(solution)/shard_map/ppermute | solution.py:29
  25.6 3.3 %collective-permute-done.8.refs_3_ = bf16[8,1536]{1,0:T(8,128)(2,1)S(1)} collective-permute-done((bf16[8,1536]{1,0:T(8,128)(2,1)S(1)}, bf16[8,1536]{1,0:T(8,128)(2,1)S(1)}, u32[]{:S(2)}, u32[]{:S(2)}) %collective-permute-start.8) | collective-permute-done | bytes 24608 | tf_op jit(solution)/shard_map/ppermute | solution.py:29
  29.0 0.6 %second_term.1 = bf16[8,1536]{1,0:T(8,128)(2,1)} custom-call(bf16[8,1536]{1,0:T(8,128)(2,1)S(1)} %get-tuple-element.8.refs_0_, bf16[8,1536]{1,0:T(8,128)(2,1)S(1)} %collective-permute-done.6.refs_1_, bf16[8,1536]{1,0:T(8,128)(2,1)S(1)} %collective-permute-done.7.refs_2_, bf16[8,1536]{1,0:T(8,128)(2,1)S(1)} %collective-permute-done.8.refs_3_, ...), custom_call_target="tpu_custom_call" | custom-call | tf_op jit(solution)/shard_map/second_term/pallas_call | solution.py:153
Async XLA Ops:
  0.6 8.2 %collective-permute-start.2 = (bf16[8,1536]{1,0:T(8,128)(2,1)}, bf16[8,1536]{1,0:T(8,128)(2,1)S(1)}, u32[]{:S(2)}, u32[]{:S(2)}) collective-permute-start(bf16[8,1536]{1,0:T(8,128)(2,1)} %bitcast.4), channel_id=1, source_target_pairs={{0,3},{1,2},{2,1},{3,0},{4,7},{5,6},{6,5},{7,4},{8,11},{9,10},{10,... | collective-permute-start | bytes 73736 | tf_op jit(solution)/shard_map/ppermute | solution.py:29
  5.7 4.9 %collective-permute-start.1 = (bf16[8,1536]{1,0:T(8,128)(2,1)}, bf16[8,1536]{1,0:T(8,128)(2,1)S(1)}, u32[]{:S(2)}, u32[]{:S(2)}) collective-permute-start(bf16[8,1536]{1,0:T(8,128)(2,1)} %bitcast.5), channel_id=1, source_target_pairs={{0,2},{1,3},{2,0},{3,1},{4,6},{5,7},{6,4},{7,5},{8,10},{9,11},{10,... | collective-permute-start | bytes 73736 | tf_op jit(solution)/shard_map/ppermute | solution.py:29
  5.7 4.9 %collective-permute-start = (bf16[8,1536]{1,0:T(8,128)(2,1)}, bf16[8,1536]{1,0:T(8,128)(2,1)S(1)}, u32[]{:S(2)}, u32[]{:S(2)}) collective-permute-start(bf16[8,1536]{1,0:T(8,128)(2,1)} %bitcast.6), channel_id=1, source_target_pairs={{0,1},{1,0},{2,3},{3,2},{4,5},{5,4},{6,7},{7,6},{8,9},{9,8},{10,11... | collective-permute-start | bytes 73736 | tf_op jit(solution)/shard_map/ppermute | solution.py:29
  7.0 3.6 %copy-start = (f32[1,6144]{1,0:T(1,128)S(1)}, f32[1,6144]{1,0:T(1,128)}, u32[]{:S(2)}) copy-start(f32[1,6144]{1,0:T(1,128)} %refs_8_.3) | copy-start | bytes 73732
  7.0 3.6 %copy-start.1 = (bf16[8,1,1,1536]{3,0,2,1:T(8,128)(2,1)S(1)}, bf16[8,1,1,1536]{3,0,2,1:T(8,128)(2,1)}, u32[]{:S(2)}) copy-start(bf16[8,1,1,1536]{3,0,2,1:T(8,128)(2,1)} %param.6) | copy-start | bytes 73732
  7.1 3.6 %copy-start.2 = (s32[1,1,8]{2,1,0:T(1,128)S(1)}, s32[1,1,8]{2,1,0:T(1,128)}, u32[]{:S(2)}) copy-start(s32[1,1,8]{2,1,0:T(1,128)} %refs_5_.3) | copy-start | bytes 100
  7.1 3.6 %copy-start.3 = (s32[1,1,8]{2,1,0:T(1,128)S(1)}, s32[1,1,8]{2,1,0:T(1,128)}, u32[]{:S(2)}) copy-start(s32[1,1,8]{2,1,0:T(1,128)} %refs_6_.3) | copy-start | bytes 100
  11.7 5.1 %collective-permute-start.5 = (bf16[8,6144]{1,0:T(8,128)(2,1)S(1)}, bf16[8,6144]{1,0:T(8,128)(2,1)S(1)}, u32[]{:S(2)}, u32[]{:S(2)}) collective-permute-start(bf16[8,6144]{1,0:T(8,128)(2,1)S(1)} %first_product.1.refs_0_), channel_id=1, source_target_pairs={{0,12},{4,8},{8,4},{12,0},{1,13},{5,9},{9,5},{13,1},{2,14},{6,10},... | collective-permute-start | bytes 294920 | tf_op jit(solution)/shard_map/ppermute | solution.py:29
  11.8 7.2 %collective-permute-start.4 = (bf16[8,6144]{1,0:T(8,128)(2,1)S(1)}, bf16[8,6144]{1,0:T(8,128)(2,1)S(1)}, u32[]{:S(2)}, u32[]{:S(2)}) collective-permute-start(bf16[8,6144]{1,0:T(8,128)(2,1)S(1)} %first_product.1.refs_0_), channel_id=1, source_target_pairs={{0,8},{4,12},{8,0},{12,4},{1,9},{5,13},{9,1},{13,5},{2,10},{6,14},... | collective-permute-start | bytes 294920 | tf_op jit(solution)/shard_map/ppermute | solution.py:29
  13.4 5.6 %collective-permute-start.3 = (bf16[8,6144]{1,0:T(8,128)(2,1)S(1)}, bf16[8,6144]{1,0:T(8,128)(2,1)S(1)}, u32[]{:S(2)}, u32[]{:S(2)}) collective-permute-start(bf16[8,6144]{1,0:T(8,128)(2,1)S(1)} %first_product.1.refs_0_), channel_id=1, source_target_pairs={{0,4},{4,0},{8,12},{12,8},{1,5},{5,1},{9,13},{13,9},{2,6},{6,2},{1... | collective-permute-start | bytes 294920 | tf_op jit(solution)/shard_map/ppermute | solution.py:29
  20.9 4.4 %collective-permute-start.6 = (bf16[8,1536]{1,0:T(8,128)(2,1)S(1)}, bf16[8,1536]{1,0:T(8,128)(2,1)S(1)}, u32[]{:S(2)}, u32[]{:S(2)}) collective-permute-start(bf16[8,1536]{1,0:T(8,128)(2,1)S(1)} %get-tuple-element.9), channel_id=1, source_target_pairs={{0,1},{1,0},{2,3},{3,2},{4,5},{5,4},{6,7},{7,6},{8,9},{9,8},{10,11... | collective-permute-start | bytes 73736 | tf_op jit(solution)/shard_map/ppermute | solution.py:29
  20.9 4.7 %collective-permute-start.7 = (bf16[8,1536]{1,0:T(8,128)(2,1)S(1)}, bf16[8,1536]{1,0:T(8,128)(2,1)S(1)}, u32[]{:S(2)}, u32[]{:S(2)}) collective-permute-start(bf16[8,1536]{1,0:T(8,128)(2,1)S(1)} %get-tuple-element.10), channel_id=1, source_target_pairs={{0,2},{1,3},{2,0},{3,1},{4,6},{5,7},{6,4},{7,5},{8,10},{9,11},{10,... | collective-permute-start | bytes 73736 | tf_op jit(solution)/shard_map/ppermute | solution.py:29
  23.4 5.6 %collective-permute-start.8 = (bf16[8,1536]{1,0:T(8,128)(2,1)S(1)}, bf16[8,1536]{1,0:T(8,128)(2,1)S(1)}, u32[]{:S(2)}, u32[]{:S(2)}) collective-permute-start(bf16[8,1536]{1,0:T(8,128)(2,1)S(1)} %get-tuple-element.11), channel_id=1, source_target_pairs={{0,3},{1,2},{2,1},{3,0},{4,7},{5,6},{6,5},{7,4},{8,11},{9,10},{10,... | collective-permute-start | bytes 73736 | tf_op jit(solution)/shard_map/ppermute | solution.py:29

commit v3 on v2

--- a/solution.py
+++ b/solution.py
@@ -29,6 +29,15 @@
         lax.ppermute(pieces[k - 1], axis, [(i, to(i, k)) for i in range(size)])
         for k in range(size - 1, 0, -1)
     ][::-1]
+
+
+def gather_pairs(part, axis, size):
+    if size & (size - 1):
+        return exchange([part] * (size - 1), axis, size)
+    swap = [(i, i ^ 1) for i in range(size)]
+    far = [lax.ppermute(part, axis, [(i, i ^ k) for i in range(size)]) for k in range(2, size, 2)]
+    near = [lax.ppermute(a, axis, swap) for a in [part] + far]
+    return near + far
 
 
 def lanes(start, length):
@@ -94,7 +103,8 @@
 
 
 def last_kernel(size, *refs):
-    parts, (noise, out) = refs[:size], refs[size:]
+    parts, (noise, first, first_out, out) = refs[:size], refs[size:]
+    first_out[...] = first[...]
     sums = parts[0][...].astype(jnp.float32)
     for part in parts[1:]:
         sums = sums + part[...].astype(jnp.float32)
@@ -139,7 +149,7 @@
         compiler_params=params,
         name="first_product",
     )(*pieces, *tables)
-    parts = [part] + exchange([part] * (n_row - 1), "row", n_row)
+    parts = [part] + gather_pairs(part, "row", n_row)
     first, *seconds = pl.pallas_call(
         functools.partial(second_kernel, n_row, n_col),
         out_shape=[row_type] + [piece_type] * n_col,
@@ -150,14 +160,14 @@
         name="second_product",
     )(*parts, *tables)
     arrived = [seconds[0]] + exchange(seconds[1:], "col", n_col)
-    second = pl.pallas_call(
+    first, second = pl.pallas_call(
         functools.partial(last_kernel, n_col),
-        out_shape=piece_type,
-        in_specs=[VMEM] * (n_col + 1),
-        out_specs=VMEM,
+        out_shape=[row_type, piece_type],
+        in_specs=[VMEM] * (n_col + 2),
+        out_specs=[VMEM] * 2,
         compiler_params=params,
         name="second_term",
-    )(*arrived, own)
+    )(*arrived[::-1], own, first)
     return first.reshape(vectors, 1, 1, -1), second.reshape(vectors, 1, 1, -1)
 
 

time: 29.8 us -> 26.7 us (0.90)
  waiting for transfers between devices: 10.9 us -> 8.67 us
  Pallas kernels: 5.24 us -> 4.75 us
  starting transfers between devices: 12.1 us -> 11.8 us
    ppermute x9 -> x6, waiting for transfers between devices: 10.9 us -> 4.25 us  [exchange(): lax.ppermute(pieces[k - 1], axis, [(i, to(i, k)) for i in range(size)])]
    ppermute x0 -> x3, waiting for transfers between devices: none -> 4.42 us  [the longest x1 3.12 us: gather_pairs(): lax.ppermute(part, axis, [(i, i ^ k) for i in range(size)])]
    ppermute x9 -> x6, starting transfers between devices: 12.1 us -> 10.2 us  [exchange(): lax.ppermute(pieces[k - 1], axis, [(i, to(i, k)) for i in range(size)])]
    ppermute x0 -> x3, starting transfers between devices: none -> 1.57 us  [the longest x1 1.56 us: gather_pairs(): lax.ppermute(part, axis, [(i, i ^ k) for i in range(size)])]
    pallas_call x1, Pallas kernels: 1.89 us -> 1.41 us  [on_device(): pl.pallas_call(functools.partial(second_kernel, n_row, n_col), out_shape=...]
where the time goes in v3:
time: 26.7 us; the launch traced here: 26.6 us
  starting transfers between devices  11.8 us (44%)
  waiting for transfers between devices  8.67 us (32%)
  Pallas kernels  4.75 us (18%)
  between operations  1.37 us (5%)
    ppermute x6, starting transfers between devices, exchange(): lax.ppermute(pieces[k - 1], axis, [(i, to(i, k)) for i in range(size)])  10.2 us
    ppermute x6, waiting for transfers between devices, exchange(): lax.ppermute(pieces[k - 1], axis, [(i, to(i, k)) for i in range(size)])  4.25 us
    ppermute x1, waiting for transfers between devices, gather_pairs(): lax.ppermute(part, axis, [(i, i ^ k) for i in range(size)])  3.12 us
    pallas_call x1, Pallas kernels, on_device(): pl.pallas_call(stage_kernel, out_shape=jax.ShapeDtypeStruct(tiles.shape,...  1.7 us
    ppermute x1, starting transfers between devices, gather_pairs(): lax.ppermute(part, axis, [(i, i ^ k) for i in range(size)])  1.56 us
    pallas_call x1, Pallas kernels, on_device(): pl.pallas_call(functools.partial(second_kernel, n_row, n_col), out_shape=...  1.41 us
    ppermute x2, waiting for transfers between devices, gather_pairs(): near = [lax.ppermute(a, axis, swap) for a in [part] + far]  1.3 us
    pallas_call x1, Pallas kernels, on_device(): pl.pallas_call(functools.partial(first_kernel, n_col), out_shape=whole_ty...  1.01 us
  transfers between devices with their start and end apart: 9, of which 5 were waited for; matrix products, arithmetic and copies ran while one was open for 0% of the time, Pallas kernels for 6%

profile of v3, /device:TPU:0, one launch (start us, length us, event | category | flops | bytes accessed | tf_op | source)
XLA Modules:
  0.0 26.6 jit_solution(4544735152711148744)
XLA Ops:
  0.6 5.1 %collective-permute-start.2 = (bf16[8,1536]{1,0:T(8,128)(2,1)}, bf16[8,1536]{1,0:T(8,128)(2,1)S(1)}, u32[]{:S(2)}, u32[]{:S(2)}) collective-permute-start(bf16[8,1536]{1,0:T(8,128)(2,1)} %bitcast.4), channel_id=1, source_target_pairs={{0,3},{1,2},{2,1},{3,0},{4,7},{5,6},{6,5},{7,4},{8,11},{9,10},{10,... | collective-permute-start | bytes 73736 | tf_op jit(solution)/shard_map/ppermute | solution.py:29
  5.7 0.0 collective-permute-start.1
  5.7 0.6 %collective-permute-start = (bf16[8,1536]{1,0:T(8,128)(2,1)}, bf16[8,1536]{1,0:T(8,128)(2,1)S(1)}, u32[]{:S(2)}, u32[]{:S(2)}) collective-permute-start(bf16[8,1536]{1,0:T(8,128)(2,1)} %bitcast.6), channel_id=1, source_target_pairs={{0,1},{1,0},{2,3},{3,2},{4,5},{5,4},{6,7},{7,6},{8,9},{9,8},{10,11... | collective-permute-start | bytes 73736 | tf_op jit(solution)/shard_map/ppermute | solution.py:29
  7.0 0.0 copy-start
  7.0 0.0 copy-start.1
  7.1 0.0 copy-start.2
  7.1 0.0 copy-start.3
  7.1 1.7 %stage.1.refs_4_ = bf16[8,384,384]{2,1,0:T(8,128)(2,1)S(1)} custom-call(bf16[8,384,384]{2,1,0:T(8,128)(2,1)} %bitcast.9), custom_call_target="tpu_custom_call" | custom-call | bytes 4718592 | tf_op jit(solution)/shard_map/stage/pallas_call | solution.py:130
  8.8 0.0 collective-permute-done.2.refs_3_
  8.8 1.9 %collective-permute-done.1.refs_2_ = bf16[8,1536]{1,0:T(8,128)(2,1)S(1)} collective-permute-done((bf16[8,1536]{1,0:T(8,128)(2,1)}, bf16[8,1536]{1,0:T(8,128)(2,1)S(1)}, u32[]{:S(2)}, u32[]{:S(2)}) %collective-permute-start.1) | collective-permute-done | bytes 24608 | tf_op jit(solution)/shard_map/ppermute | solution.py:29
  10.7 0.0 collective-permute-done.refs_1_
  10.7 0.0 copy-done
  10.7 0.0 copy-done.1
  10.7 0.0 copy-done.2
  10.7 0.0 copy-done.3
  10.7 1.0 %first_product.1.refs_0_ = bf16[8,6144]{1,0:T(8,128)(2,1)S(1)} custom-call(bf16[8,1536]{1,0:T(8,128)(2,1)S(1)} %bitcast.7, bf16[8,1536]{1,0:T(8,128)(2,1)S(1)} %collective-permute-done.refs_1_, bf16[8,1536]{1,0:T(8,128)(2,1)S(1)} %collective-permute-done.1.refs_2_, bf16[8,1536]{1,0:T(8,128)(2,1)S(1)} %collective-permute-done.2.refs_3_, ...), custom_call_target="tpu_custom_call" | custom-call | tf_op jit(solution)/shard_map/first_product/pallas_call | solution.py:143
  11.7 1.6 %collective-permute-start.4 = (bf16[8,6144]{1,0:T(8,128)(2,1)S(1)}, bf16[8,6144]{1,0:T(8,128)(2,1)S(1)}, u32[]{:S(2)}, u32[]{:S(2)}) collective-permute-start(bf16[8,6144]{1,0:T(8,128)(2,1)S(1)} %first_product.1.refs_0_), channel_id=1, source_target_pairs={{0,8},{4,12},{8,0},{12,4},{1,9},{5,13},{9,1},{13,5},{2,10},{6,14},... | collective-permute-start | bytes 294920 | tf_op jit(solution)/shard_map/ppermute | solution.py:38
  13.3 0.0 collective-permute-start.3
  13.3 3.1 %collective-permute-done.4.refs_3_ = bf16[8,6144]{1,0:T(8,128)(2,1)S(1)} collective-permute-done((bf16[8,6144]{1,0:T(8,128)(2,1)S(1)}, bf16[8,6144]{1,0:T(8,128)(2,1)S(1)}, u32[]{:S(2)}, u32[]{:S(2)}) %collective-permute-start.4) | collective-permute-done | bytes 98336 | tf_op jit(solution)/shard_map/ppermute | solution.py:38
  16.4 0.0 collective-permute-start.5
  16.4 0.0 collective-permute-done.3.refs_1_
  16.4 1.3 %collective-permute-done.5.refs_2_ = bf16[8,6144]{1,0:T(8,128)(2,1)S(1)} collective-permute-done((bf16[8,6144]{1,0:T(8,128)(2,1)S(1)}, bf16[8,6144]{1,0:T(8,128)(2,1)S(1)}, u32[]{:S(2)}, u32[]{:S(2)}) %collective-permute-start.5) | collective-permute-done | bytes 98336 | tf_op jit(solution)/shard_map/ppermute | solution.py:39
  17.7 1.4 %second_product.1 = (bf16[8,1536]{1,0:T(8,128)(2,1)S(1)}, bf16[8,1536]{1,0:T(8,128)(2,1)S(1)}, bf16[8,1536]{1,0:T(8,128)(2,1)S(1)}, bf16[8,1536]{1,0:T(8,128)(2,1)S(1)}, bf16[8,1536]{1,0:T(8,128)(2,1)S(1)}) custom-call(bf16[8,6144]{1,0:T(8,128)(2,1)S(1)} %first_product.1.refs_0_, bf16[8,6144]{1,0:T(8,128)(2,1)S(1)} %collective-permute-done.3.refs_1_, ...), custom_call_target="tpu_custom_call" | custom-call | tf_op jit(solution)/shard_map/second_product/pallas_call | solution.py:153
  19.1 2.0 %collective-permute-start.6 = (bf16[8,1536]{1,0:T(8,128)(2,1)S(1)}, bf16[8,1536]{1,0:T(8,128)(2,1)S(1)}, u32[]{:S(2)}, u32[]{:S(2)}) collective-permute-start(bf16[8,1536]{1,0:T(8,128)(2,1)S(1)} %get-tuple-element.9), channel_id=1, source_target_pairs={{0,3},{1,2},{2,1},{3,0},{4,7},{5,6},{6,5},{7,4},{8,11},{9,10},{10,... | collective-permute-start | bytes 73736 | tf_op jit(solution)/shard_map/ppermute | solution.py:29
  21.1 0.2 collective-permute-start.7
  21.3 2.3 %collective-permute-start.8 = (bf16[8,1536]{1,0:T(8,128)(2,1)S(1)}, bf16[8,1536]{1,0:T(8,128)(2,1)S(1)}, u32[]{:S(2)}, u32[]{:S(2)}) collective-permute-start(bf16[8,1536]{1,0:T(8,128)(2,1)S(1)} %get-tuple-element.11), channel_id=1, source_target_pairs={{0,1},{1,0},{2,3},{3,2},{4,5},{5,4},{6,7},{7,6},{8,9},{9,8},{10,11... | collective-permute-start | bytes 73736 | tf_op jit(solution)/shard_map/ppermute | solution.py:29
  23.6 1.6 %collective-permute-done.6.refs_0_ = bf16[8,1536]{1,0:T(8,128)(2,1)S(1)} collective-permute-done((bf16[8,1536]{1,0:T(8,128)(2,1)S(1)}, bf16[8,1536]{1,0:T(8,128)(2,1)S(1)}, u32[]{:S(2)}, u32[]{:S(2)}) %collective-permute-start.6) | collective-permute-done | bytes 24608 | tf_op jit(solution)/shard_map/ppermute | solution.py:29
  25.2 0.8 %collective-permute-done.7.refs_1_ = bf16[8,1536]{1,0:T(8,128)(2,1)S(1)} collective-permute-done((bf16[8,1536]{1,0:T(8,128)(2,1)S(1)}, bf16[8,1536]{1,0:T(8,128)(2,1)S(1)}, u32[]{:S(2)}, u32[]{:S(2)}) %collective-permute-start.7) | collective-permute-done | bytes 24608 | tf_op jit(solution)/shard_map/ppermute | solution.py:29
  25.9 0.0 collective-permute-done.8.refs_2_
  26.0 0.6 %second_term.1 = (bf16[8,1536]{1,0:T(8,128)(2,1)}, bf16[8,1536]{1,0:T(8,128)(2,1)}) custom-call(bf16[8,1536]{1,0:T(8,128)(2,1)S(1)} %collective-permute-done.6.refs_0_, bf16[8,1536]{1,0:T(8,128)(2,1)S(1)} %collective-permute-done.7.refs_1_, bf16[8,1536]{1,0:T(8,128)(2,1)S(1)} %collective-permute-done.8.refs_2_, ...), custom_call_target="tpu_custom_call" | custom-call | tf_op jit(solution)/shard_map/second_term/pallas_call | solution.py:163
Async XLA Ops:
  0.6 8.2 %collective-permute-start.2 = (bf16[8,1536]{1,0:T(8,128)(2,1)}, bf16[8,1536]{1,0:T(8,128)(2,1)S(1)}, u32[]{:S(2)}, u32[]{:S(2)}) collective-permute-start(bf16[8,1536]{1,0:T(8,128)(2,1)} %bitcast.4), channel_id=1, source_target_pairs={{0,3},{1,2},{2,1},{3,0},{4,7},{5,6},{6,5},{7,4},{8,11},{9,10},{10,... | collective-permute-start | bytes 73736 | tf_op jit(solution)/shard_map/ppermute | solution.py:29
  5.7 4.9 %collective-permute-start.1 = (bf16[8,1536]{1,0:T(8,128)(2,1)}, bf16[8,1536]{1,0:T(8,128)(2,1)S(1)}, u32[]{:S(2)}, u32[]{:S(2)}) collective-permute-start(bf16[8,1536]{1,0:T(8,128)(2,1)} %bitcast.5), channel_id=1, source_target_pairs={{0,2},{1,3},{2,0},{3,1},{4,6},{5,7},{6,4},{7,5},{8,10},{9,11},{10,... | collective-permute-start | bytes 73736 | tf_op jit(solution)/shard_map/ppermute | solution.py:29
  5.7 4.9 %collective-permute-start = (bf16[8,1536]{1,0:T(8,128)(2,1)}, bf16[8,1536]{1,0:T(8,128)(2,1)S(1)}, u32[]{:S(2)}, u32[]{:S(2)}) collective-permute-start(bf16[8,1536]{1,0:T(8,128)(2,1)} %bitcast.6), channel_id=1, source_target_pairs={{0,1},{1,0},{2,3},{3,2},{4,5},{5,4},{6,7},{7,6},{8,9},{9,8},{10,11... | collective-permute-start | bytes 73736 | tf_op jit(solution)/shard_map/ppermute | solution.py:29
  7.0 3.6 %copy-start = (f32[1,6144]{1,0:T(1,128)S(1)}, f32[1,6144]{1,0:T(1,128)}, u32[]{:S(2)}) copy-start(f32[1,6144]{1,0:T(1,128)} %refs_8_.3) | copy-start | bytes 73732
  7.0 3.6 %copy-start.1 = (bf16[8,1,1,1536]{3,0,2,1:T(8,128)(2,1)S(1)}, bf16[8,1,1,1536]{3,0,2,1:T(8,128)(2,1)}, u32[]{:S(2)}) copy-start(bf16[8,1,1,1536]{3,0,2,1:T(8,128)(2,1)} %param.6) | copy-start | bytes 73732
  7.1 3.6 %copy-start.2 = (s32[1,1,8]{2,1,0:T(1,128)S(1)}, s32[1,1,8]{2,1,0:T(1,128)}, u32[]{:S(2)}) copy-start(s32[1,1,8]{2,1,0:T(1,128)} %refs_5_.3) | copy-start | bytes 100
  7.1 3.6 %copy-start.3 = (s32[1,1,8]{2,1,0:T(1,128)S(1)}, s32[1,1,8]{2,1,0:T(1,128)}, u32[]{:S(2)}) copy-start(s32[1,1,8]{2,1,0:T(1,128)} %refs_6_.3) | copy-start | bytes 100
  11.7 4.7 %collective-permute-start.4 = (bf16[8,6144]{1,0:T(8,128)(2,1)S(1)}, bf16[8,6144]{1,0:T(8,128)(2,1)S(1)}, u32[]{:S(2)}, u32[]{:S(2)}) collective-permute-start(bf16[8,6144]{1,0:T(8,128)(2,1)S(1)} %first_product.1.refs_0_), channel_id=1, source_target_pairs={{0,8},{4,12},{8,0},{12,4},{1,9},{5,13},{9,1},{13,5},{2,10},{6,14},... | collective-permute-start | bytes 294920 | tf_op jit(solution)/shard_map/ppermute | solution.py:38
  13.3 3.1 %collective-permute-start.3 = (bf16[8,6144]{1,0:T(8,128)(2,1)S(1)}, bf16[8,6144]{1,0:T(8,128)(2,1)S(1)}, u32[]{:S(2)}, u32[]{:S(2)}) collective-permute-start(bf16[8,6144]{1,0:T(8,128)(2,1)S(1)} %first_product.1.refs_0_), channel_id=1, source_target_pairs={{0,4},{4,0},{8,12},{12,8},{1,5},{5,1},{9,13},{13,9},{2,6},{6,2},{1... | collective-permute-start | bytes 294920 | tf_op jit(solution)/shard_map/ppermute | solution.py:39
  16.4 1.3 %collective-permute-start.5 = (bf16[8,6144]{1,0:T(8,128)(2,1)S(1)}, bf16[8,6144]{1,0:T(8,128)(2,1)S(1)}, u32[]{:S(2)}, u32[]{:S(2)}) collective-permute-start(bf16[8,6144]{1,0:T(8,128)(2,1)S(1)} %collective-permute-done.4.refs_3_), channel_id=1, source_target_pairs={{0,4},{4,0},{8,12},{12,8},{1,5},{5,1},{9,13},{13,9},{2,6},{6,2},{1... | collective-permute-start | bytes 294920 | tf_op jit(solution)/shard_map/ppermute | solution.py:39
  19.1 6.0 %collective-permute-start.6 = (bf16[8,1536]{1,0:T(8,128)(2,1)S(1)}, bf16[8,1536]{1,0:T(8,128)(2,1)S(1)}, u32[]{:S(2)}, u32[]{:S(2)}) collective-permute-start(bf16[8,1536]{1,0:T(8,128)(2,1)S(1)} %get-tuple-element.9), channel_id=1, source_target_pairs={{0,3},{1,2},{2,1},{3,0},{4,7},{5,6},{6,5},{7,4},{8,11},{9,10},{10,... | collective-permute-start | bytes 73736 | tf_op jit(solution)/shard_map/ppermute | solution.py:29
  21.1 4.9 %collective-permute-start.7 = (bf16[8,1536]{1,0:T(8,128)(2,1)S(1)}, bf16[8,1536]{1,0:T(8,128)(2,1)S(1)}, u32[]{:S(2)}, u32[]{:S(2)}) collective-permute-start(bf16[8,1536]{1,0:T(8,128)(2,1)S(1)} %get-tuple-element.10), channel_id=1, source_target_pairs={{0,2},{1,3},{2,0},{3,1},{4,6},{5,7},{6,4},{7,5},{8,10},{9,11},{10,... | collective-permute-start | bytes 73736 | tf_op jit(solution)/shard_map/ppermute | solution.py:29
  21.3 4.7 %collective-permute-start.8 = (bf16[8,1536]{1,0:T(8,128)(2,1)S(1)}, bf16[8,1536]{1,0:T(8,128)(2,1)S(1)}, u32[]{:S(2)}, u32[]{:S(2)}) collective-permute-start(bf16[8,1536]{1,0:T(8,128)(2,1)S(1)} %get-tuple-element.11), channel_id=1, source_target_pairs={{0,1},{1,0},{2,3},{3,2},{4,5},{5,4},{6,7},{7,6},{8,9},{9,8},{10,11... | collective-permute-start | bytes 73736 | tf_op jit(solution)/shard_map/ppermute | solution.py:29

commit v4 on v3

--- a/solution.py
+++ b/solution.py
@@ -14,7 +14,6 @@
 
 VMEM = pl.BlockSpec(memory_space=pltpu.VMEM)
 HBM = pl.BlockSpec(memory_space=pltpu.HBM)
-SMEM = pl.BlockSpec(memory_space=pltpu.SMEM)
 
 
 def pairing(size):
@@ -44,17 +43,14 @@
     return pl.ds(pl.multiple_of(start, 128), length)
 
 
-def add_slots(source, total, tiles, read_at, write_at, count, contract):
+def add_slots(source, total, tiles, read_at, write_at, count):
     slots, span, _ = tiles.shape
-    live, spare = count[0, 0], source.shape[1] // span
+    live, spare = count[...][0, 0], source.shape[1] // span
+    read_at, write_at = read_at[...], write_at[...]
     products = []
     for s in range(slots):
         picked = source[:, lanes(read_at[0, 0, s] * span, span)]
-        products.append(
-            lax.dot_general(
-                picked, tiles[s], (((1,), (contract,)), ((), ())), preferred_element_type=jnp.float32
-            )
-        )
+        products.append(jnp.dot(picked, tiles[s], preferred_element_type=jnp.float32))
     for s in range(slots):
         at = lanes(jnp.where(s < live, write_at[0, 0, s], spare) * span, span)
         total[:, at] += products[s]
@@ -70,6 +66,11 @@
     copy.wait()
 
 
+def turn_kernel(tiles, turned):
+    for s in range(tiles.shape[0]):
+        turned[s] = tiles[s].T
+
+
 def first_kernel(size, *refs):
     pieces, (tiles, rows, cols, count, mobility, out, whole, total) = refs[:size], refs[size:]
     _, source_of = pairing(size)
@@ -78,7 +79,7 @@
     for k in range(size):
         whole[:, lanes(source_of(me, k) * piece, piece)] = pieces[k][...]
     total[:, :group_len] = self_factor() * (mobility[...] - SHIFT) * whole[...].astype(jnp.float32)
-    add_slots(whole, total, tiles, rows, cols, count, 0)
+    add_slots(whole, total, tiles, rows, cols, count)
     out[...] = total[:, :group_len].astype(out.dtype)
 
 
@@ -94,7 +95,7 @@
     row_piece = first.shape[1]
     first[...] = whole[:, lanes(lax.axis_index("row") * row_piece, row_piece)]
     total[:, :group_len] = self_factor() * (mobility[...] - SHIFT) * whole[...].astype(jnp.float32)
-    add_slots(whole, total, tiles, cols, rows, count, 1)
+    add_slots(whole, total, tiles, cols, rows, count)
     to, _ = pairing(n_col)
     me = lax.axis_index("col")
     piece = outs[0].shape[1]
@@ -137,8 +138,17 @@
         cost_estimate=pl.CostEstimate(flops=0, transcendentals=0, bytes_accessed=4 * tiles.size),
         name="stage",
     )(tiles)
+    turned = pl.pallas_call(
+        turn_kernel,
+        out_shape=jax.ShapeDtypeStruct(tiles.shape, tiles.dtype),
+        in_specs=[VMEM],
+        out_specs=VMEM,
+        compiler_params=params,
+        cost_estimate=pl.CostEstimate(flops=0, transcendentals=0, bytes_accessed=4 * tiles.size),
+        name="turn",
+    )(staged)
     tables = (staged, block_rows, block_cols, block_count, self_mobility)
-    table_specs = [VMEM, SMEM, SMEM, SMEM, VMEM]
+    table_specs = [VMEM, VMEM, VMEM, VMEM, VMEM]
     pieces = [own] + arrived
     part = pl.pallas_call(
         functools.partial(first_kernel, n_col),
@@ -158,7 +168,7 @@
         scratch_shapes=scratch,
         compiler_params=params,
         name="second_product",
-    )(*parts, *tables)
+    )(*parts, turned, *tables[1:])
     arrived = [seconds[0]] + exchange(seconds[1:], "col", n_col)
     first, second = pl.pallas_call(
         functools.partial(last_kernel, n_col),

time: 26.7 us -> 25.4 us (0.951)
  Pallas kernels: 4.75 us -> 4.06 us
  waiting for transfers between devices: 8.67 us -> 8 us
    pallas_call x1, Pallas kernels: 1.41 us -> 0.56 us  [on_device(): pl.pallas_call(functools.partial(second_kernel, n_row, n_col), out_shape=...]
    ppermute x2, waiting for transfers between devices: 1.3 us -> 0.63 us  [gather_pairs(): near = [lax.ppermute(a, axis, swap) for a in [part] + far]]
    pallas_call x0 -> x1, Pallas kernels: none -> 0.65 us  [on_device(): pl.pallas_call(turn_kernel, out_shape=jax.ShapeDtypeStruct(tiles.shape, t...]
    pallas_call x1, Pallas kernels: 1.01 us -> 0.52 us  [on_device(): pl.pallas_call(functools.partial(first_kernel, n_col), out_shape=whole_ty...]
  transfers between devices with their start and end apart: 9 -> 9, of which waited for: 5 -> 5; matrix products, arithmetic and copies ran while one was open for 0% -> 0% of each run, Pallas kernels for 6% -> 9%
where the time goes in v4:
time: 25.4 us; the launch traced here: 25.2 us
  starting transfers between devices  11.8 us (46%)
  waiting for transfers between devices  8 us (31%)
  Pallas kernels  4.06 us (16%)
  between operations  1.39 us (5%)
    ppermute x6, starting transfers between devices, exchange(): lax.ppermute(pieces[k - 1], axis, [(i, to(i, k)) for i in range(size)])  10.2 us
    ppermute x6, waiting for transfers between devices, exchange(): lax.ppermute(pieces[k - 1], axis, [(i, to(i, k)) for i in range(size)])  4.25 us
    ppermute x1, waiting for transfers between devices, gather_pairs(): lax.ppermute(part, axis, [(i, i ^ k) for i in range(size)])  3.12 us
    pallas_call x1, Pallas kernels, on_device(): pl.pallas_call(stage_kernel, out_shape=jax.ShapeDtypeStruct(tiles.shape,...  1.7 us
    ppermute x1, starting transfers between devices, gather_pairs(): lax.ppermute(part, axis, [(i, i ^ k) for i in range(size)])  1.56 us
    pallas_call x1, Pallas kernels, on_device(): pl.pallas_call(turn_kernel, out_shape=jax.ShapeDtypeStruct(tiles.shape, t...  0.65 us
    pallas_call x1, Pallas kernels, on_device(): pl.pallas_call(functools.partial(last_kernel, n_col), out_shape=[row_type...  0.63 us
    ppermute x2, waiting for transfers between devices, gather_pairs(): near = [lax.ppermute(a, axis, swap) for a in [part] + far]  0.63 us
  transfers between devices with their start and end apart: 9, of which 5 were waited for; matrix products, arithmetic and copies ran while one was open for 0% of the time, Pallas kernels for 9%

profile of v4, /device:TPU:0, one launch (start us, length us, event | category | flops | bytes accessed | tf_op | source)
XLA Modules:
  0.0 25.2 jit_solution(6088511734428333049)
XLA Ops:
  0.6 5.1 %collective-permute-start.2 = (bf16[8,1536]{1,0:T(8,128)(2,1)}, bf16[8,1536]{1,0:T(8,128)(2,1)S(1)}, u32[]{:S(2)}, u32[]{:S(2)}) collective-permute-start(bf16[8,1536]{1,0:T(8,128)(2,1)} %bitcast.4), channel_id=1, source_target_pairs={{0,3},{1,2},{2,1},{3,0},{4,7},{5,6},{6,5},{7,4},{8,11},{9,10},{10,... | collective-permute-start | bytes 73736 | tf_op jit(solution)/shard_map/ppermute | solution.py:28
  5.7 0.0 collective-permute-start.1
  5.7 0.6 %collective-permute-start = (bf16[8,1536]{1,0:T(8,128)(2,1)}, bf16[8,1536]{1,0:T(8,128)(2,1)S(1)}, u32[]{:S(2)}, u32[]{:S(2)}) collective-permute-start(bf16[8,1536]{1,0:T(8,128)(2,1)} %bitcast.6), channel_id=1, source_target_pairs={{0,1},{1,0},{2,3},{3,2},{4,5},{5,4},{6,7},{7,6},{8,9},{9,8},{10,11... | collective-permute-start | bytes 73736 | tf_op jit(solution)/shard_map/ppermute | solution.py:28
  7.0 0.0 copy-start
  7.0 0.0 copy-start.1
  7.1 0.0 copy-start.2
  7.1 0.0 copy-start.3
  7.1 1.7 %stage.1.refs_4_.tiles = bf16[8,384,384]{2,1,0:T(8,128)(2,1)S(1)} custom-call(bf16[8,384,384]{2,1,0:T(8,128)(2,1)} %bitcast.9), custom_call_target="tpu_custom_call" | custom-call | bytes 4718592 | tf_op jit(solution)/shard_map/stage/pallas_call | solution.py:131
  8.8 0.0 collective-permute-done.2.refs_3_
  8.8 1.9 %collective-permute-done.1.refs_2_ = bf16[8,1536]{1,0:T(8,128)(2,1)S(1)} collective-permute-done((bf16[8,1536]{1,0:T(8,128)(2,1)}, bf16[8,1536]{1,0:T(8,128)(2,1)S(1)}, u32[]{:S(2)}, u32[]{:S(2)}) %collective-permute-start.1) | collective-permute-done | bytes 24608 | tf_op jit(solution)/shard_map/ppermute | solution.py:28
  10.7 0.0 collective-permute-done.refs_1_
  10.7 0.0 copy-done
  10.7 0.0 copy-done.1
  10.7 0.0 copy-done.2
  10.7 0.0 copy-done.3
  10.7 0.5 %first_product.1.refs_0_ = bf16[8,6144]{1,0:T(8,128)(2,1)S(1)} custom-call(bf16[8,1536]{1,0:T(8,128)(2,1)S(1)} %bitcast.7, bf16[8,1536]{1,0:T(8,128)(2,1)S(1)} %collective-permute-done.refs_1_, bf16[8,1536]{1,0:T(8,128)(2,1)S(1)} %collective-permute-done.1.refs_2_, bf16[8,1536]{1,0:T(8,128)(2,1)S(1)} %collective-permute-done.2.refs_3_, ...), custom_call_target="tpu_custom_call" | custom-call | tf_op jit(solution)/shard_map/first_product/pallas_call | solution.py:153
  11.2 1.6 %collective-permute-start.4 = (bf16[8,6144]{1,0:T(8,128)(2,1)S(1)}, bf16[8,6144]{1,0:T(8,128)(2,1)S(1)}, u32[]{:S(2)}, u32[]{:S(2)}) collective-permute-start(bf16[8,6144]{1,0:T(8,128)(2,1)S(1)} %first_product.1.refs_0_), channel_id=1, source_target_pairs={{0,8},{4,12},{8,0},{12,4},{1,9},{5,13},{9,1},{13,5},{2,10},{6,14},... | collective-permute-start | bytes 294920 | tf_op jit(solution)/shard_map/ppermute | solution.py:37
  12.8 0.0 collective-permute-start.3
  12.8 3.1 %collective-permute-done.4.refs_3_ = bf16[8,6144]{1,0:T(8,128)(2,1)S(1)} collective-permute-done((bf16[8,6144]{1,0:T(8,128)(2,1)S(1)}, bf16[8,6144]{1,0:T(8,128)(2,1)S(1)}, u32[]{:S(2)}, u32[]{:S(2)}) %collective-permute-start.4) | collective-permute-done | bytes 98336 | tf_op jit(solution)/shard_map/ppermute | solution.py:37
  15.9 0.0 collective-permute-start.5
  15.9 0.7 %turn.1.refs_4_ = bf16[8,384,384]{2,1,0:T(8,128)(2,1)S(1)} custom-call(bf16[8,384,384]{2,1,0:T(8,128)(2,1)S(1)} %stage.1.refs_4_.tiles), custom_call_target="tpu_custom_call" | custom-call | bytes 4718592 | tf_op jit(solution)/shard_map/turn/pallas_call | solution.py:141
  16.6 0.0 collective-permute-done.3.refs_1_
  16.6 0.6 %collective-permute-done.5.refs_2_ = bf16[8,6144]{1,0:T(8,128)(2,1)S(1)} collective-permute-done((bf16[8,6144]{1,0:T(8,128)(2,1)S(1)}, bf16[8,6144]{1,0:T(8,128)(2,1)S(1)}, u32[]{:S(2)}, u32[]{:S(2)}) %collective-permute-start.5) | collective-permute-done | bytes 98336 | tf_op jit(solution)/shard_map/ppermute | solution.py:38
  17.2 0.6 %second_product.1 = (bf16[8,1536]{1,0:T(8,128)(2,1)S(1)}, bf16[8,1536]{1,0:T(8,128)(2,1)S(1)}, bf16[8,1536]{1,0:T(8,128)(2,1)S(1)}, bf16[8,1536]{1,0:T(8,128)(2,1)S(1)}, bf16[8,1536]{1,0:T(8,128)(2,1)S(1)}) custom-call(bf16[8,6144]{1,0:T(8,128)(2,1)S(1)} %first_product.1.refs_0_, bf16[8,6144]{1,0:T(8,128)(2,1)S(1)} %collective-permute-done.3.refs_1_, ...), custom_call_target="tpu_custom_call" | custom-call | tf_op jit(solution)/shard_map/second_product/pallas_call | solution.py:163
  17.8 2.0 %collective-permute-start.6 = (bf16[8,1536]{1,0:T(8,128)(2,1)S(1)}, bf16[8,1536]{1,0:T(8,128)(2,1)S(1)}, u32[]{:S(2)}, u32[]{:S(2)}) collective-permute-start(bf16[8,1536]{1,0:T(8,128)(2,1)S(1)} %get-tuple-element.9), channel_id=1, source_target_pairs={{0,3},{1,2},{2,1},{3,0},{4,7},{5,6},{6,5},{7,4},{8,11},{9,10},{10,... | collective-permute-start | bytes 73736 | tf_op jit(solution)/shard_map/ppermute | solution.py:28
  19.7 0.2 collective-permute-start.7
  20.0 2.3 %collective-permute-start.8 = (bf16[8,1536]{1,0:T(8,128)(2,1)S(1)}, bf16[8,1536]{1,0:T(8,128)(2,1)S(1)}, u32[]{:S(2)}, u32[]{:S(2)}) collective-permute-start(bf16[8,1536]{1,0:T(8,128)(2,1)S(1)} %get-tuple-element.11), channel_id=1, source_target_pairs={{0,1},{1,0},{2,3},{3,2},{4,5},{5,4},{6,7},{7,6},{8,9},{9,8},{10,11... | collective-permute-start | bytes 73736 | tf_op jit(solution)/shard_map/ppermute | solution.py:28
  22.2 1.6 %collective-permute-done.6.refs_0_ = bf16[8,1536]{1,0:T(8,128)(2,1)S(1)} collective-permute-done((bf16[8,1536]{1,0:T(8,128)(2,1)S(1)}, bf16[8,1536]{1,0:T(8,128)(2,1)S(1)}, u32[]{:S(2)}, u32[]{:S(2)}) %collective-permute-start.6) | collective-permute-done | bytes 24608 | tf_op jit(solution)/shard_map/ppermute | solution.py:28
  23.8 0.8 %collective-permute-done.7.refs_1_ = bf16[8,1536]{1,0:T(8,128)(2,1)S(1)} collective-permute-done((bf16[8,1536]{1,0:T(8,128)(2,1)S(1)}, bf16[8,1536]{1,0:T(8,128)(2,1)S(1)}, u32[]{:S(2)}, u32[]{:S(2)}) %collective-permute-start.7) | collective-permute-done | bytes 24608 | tf_op jit(solution)/shard_map/ppermute | solution.py:28
  24.6 0.0 collective-permute-done.8.refs_2_
  24.6 0.6 %second_term.1 = (bf16[8,1536]{1,0:T(8,128)(2,1)}, bf16[8,1536]{1,0:T(8,128)(2,1)}) custom-call(bf16[8,1536]{1,0:T(8,128)(2,1)S(1)} %collective-permute-done.6.refs_0_, bf16[8,1536]{1,0:T(8,128)(2,1)S(1)} %collective-permute-done.7.refs_1_, bf16[8,1536]{1,0:T(8,128)(2,1)S(1)} %collective-permute-done.8.refs_2_, ...), custom_call_target="tpu_custom_call" | custom-call | tf_op jit(solution)/shard_map/second_term/pallas_call | solution.py:173
Async XLA Ops:
  0.6 8.2 %collective-permute-start.2 = (bf16[8,1536]{1,0:T(8,128)(2,1)}, bf16[8,1536]{1,0:T(8,128)(2,1)S(1)}, u32[]{:S(2)}, u32[]{:S(2)}) collective-permute-start(bf16[8,1536]{1,0:T(8,128)(2,1)} %bitcast.4), channel_id=1, source_target_pairs={{0,3},{1,2},{2,1},{3,0},{4,7},{5,6},{6,5},{7,4},{8,11},{9,10},{10,... | collective-permute-start | bytes 73736 | tf_op jit(solution)/shard_map/ppermute | solution.py:28
  5.7 4.9 %collective-permute-start.1 = (bf16[8,1536]{1,0:T(8,128)(2,1)}, bf16[8,1536]{1,0:T(8,128)(2,1)S(1)}, u32[]{:S(2)}, u32[]{:S(2)}) collective-permute-start(bf16[8,1536]{1,0:T(8,128)(2,1)} %bitcast.5), channel_id=1, source_target_pairs={{0,2},{1,3},{2,0},{3,1},{4,6},{5,7},{6,4},{7,5},{8,10},{9,11},{10,... | collective-permute-start | bytes 73736 | tf_op jit(solution)/shard_map/ppermute | solution.py:28
  5.7 4.9 %collective-permute-start = (bf16[8,1536]{1,0:T(8,128)(2,1)}, bf16[8,1536]{1,0:T(8,128)(2,1)S(1)}, u32[]{:S(2)}, u32[]{:S(2)}) collective-permute-start(bf16[8,1536]{1,0:T(8,128)(2,1)} %bitcast.6), channel_id=1, source_target_pairs={{0,1},{1,0},{2,3},{3,2},{4,5},{5,4},{6,7},{7,6},{8,9},{9,8},{10,11... | collective-permute-start | bytes 73736 | tf_op jit(solution)/shard_map/ppermute | solution.py:28
  7.0 3.6 %copy-start = (f32[1,6144]{1,0:T(1,128)S(1)}, f32[1,6144]{1,0:T(1,128)}, u32[]{:S(2)}) copy-start(f32[1,6144]{1,0:T(1,128)} %refs_8_.3) | copy-start | bytes 73732
  7.0 3.6 %copy-start.1 = (bf16[8,1,1,1536]{3,0,2,1:T(8,128)(2,1)S(1)}, bf16[8,1,1,1536]{3,0,2,1:T(8,128)(2,1)}, u32[]{:S(2)}) copy-start(bf16[8,1,1,1536]{3,0,2,1:T(8,128)(2,1)} %param.6) | copy-start | bytes 73732
  7.1 3.6 %copy-start.2 = (s32[1,1,8]{2,1,0:T(1,128)S(1)}, s32[1,1,8]{2,1,0:T(1,128)}, u32[]{:S(2)}) copy-start(s32[1,1,8]{2,1,0:T(1,128)} %refs_5_.3) | copy-start | bytes 100
  7.1 3.6 %copy-start.3 = (s32[1,1,8]{2,1,0:T(1,128)S(1)}, s32[1,1,8]{2,1,0:T(1,128)}, u32[]{:S(2)}) copy-start(s32[1,1,8]{2,1,0:T(1,128)} %refs_6_.3) | copy-start | bytes 100
  11.2 4.7 %collective-permute-start.4 = (bf16[8,6144]{1,0:T(8,128)(2,1)S(1)}, bf16[8,6144]{1,0:T(8,128)(2,1)S(1)}, u32[]{:S(2)}, u32[]{:S(2)}) collective-permute-start(bf16[8,6144]{1,0:T(8,128)(2,1)S(1)} %first_product.1.refs_0_), channel_id=1, source_target_pairs={{0,8},{4,12},{8,0},{12,4},{1,9},{5,13},{9,1},{13,5},{2,10},{6,14},... | collective-permute-start | bytes 294920 | tf_op jit(solution)/shard_map/ppermute | solution.py:37
  12.8 3.8 %collective-permute-start.3 = (bf16[8,6144]{1,0:T(8,128)(2,1)S(1)}, bf16[8,6144]{1,0:T(8,128)(2,1)S(1)}, u32[]{:S(2)}, u32[]{:S(2)}) collective-permute-start(bf16[8,6144]{1,0:T(8,128)(2,1)S(1)} %first_product.1.refs_0_), channel_id=1, source_target_pairs={{0,4},{4,0},{8,12},{12,8},{1,5},{5,1},{9,13},{13,9},{2,6},{6,2},{1... | collective-permute-start | bytes 294920 | tf_op jit(solution)/shard_map/ppermute | solution.py:38
  15.9 1.3 %collective-permute-start.5 = (bf16[8,6144]{1,0:T(8,128)(2,1)S(1)}, bf16[8,6144]{1,0:T(8,128)(2,1)S(1)}, u32[]{:S(2)}, u32[]{:S(2)}) collective-permute-start(bf16[8,6144]{1,0:T(8,128)(2,1)S(1)} %collective-permute-done.4.refs_3_), channel_id=1, source_target_pairs={{0,4},{4,0},{8,12},{12,8},{1,5},{5,1},{9,13},{13,9},{2,6},{6,2},{1... | collective-permute-start | bytes 294920 | tf_op jit(solution)/shard_map/ppermute | solution.py:38
  17.8 6.0 %collective-permute-start.6 = (bf16[8,1536]{1,0:T(8,128)(2,1)S(1)}, bf16[8,1536]{1,0:T(8,128)(2,1)S(1)}, u32[]{:S(2)}, u32[]{:S(2)}) collective-permute-start(bf16[8,1536]{1,0:T(8,128)(2,1)S(1)} %get-tuple-element.9), channel_id=1, source_target_pairs={{0,3},{1,2},{2,1},{3,0},{4,7},{5,6},{6,5},{7,4},{8,11},{9,10},{10,... | collective-permute-start | bytes 73736 | tf_op jit(solution)/shard_map/ppermute | solution.py:28
  19.7 4.9 %collective-permute-start.7 = (bf16[8,1536]{1,0:T(8,128)(2,1)S(1)}, bf16[8,1536]{1,0:T(8,128)(2,1)S(1)}, u32[]{:S(2)}, u32[]{:S(2)}) collective-permute-start(bf16[8,1536]{1,0:T(8,128)(2,1)S(1)} %get-tuple-element.10), channel_id=1, source_target_pairs={{0,2},{1,3},{2,0},{3,1},{4,6},{5,7},{6,4},{7,5},{8,10},{9,11},{10,... | collective-permute-start | bytes 73736 | tf_op jit(solution)/shard_map/ppermute | solution.py:28
  20.0 4.7 %collective-permute-start.8 = (bf16[8,1536]{1,0:T(8,128)(2,1)S(1)}, bf16[8,1536]{1,0:T(8,128)(2,1)S(1)}, u32[]{:S(2)}, u32[]{:S(2)}) collective-permute-start(bf16[8,1536]{1,0:T(8,128)(2,1)S(1)} %get-tuple-element.11), channel_id=1, source_target_pairs={{0,1},{1,0},{2,3},{3,2},{4,5},{5,4},{6,7},{7,6},{8,9},{9,8},{10,11... | collective-permute-start | bytes 73736 | tf_op jit(solution)/shard_map/ppermute | solution.py:28

commit v5 on v4

--- a/solution.py
+++ b/solution.py
@@ -16,23 +16,35 @@
 HBM = pl.BlockSpec(memory_space=pltpu.HBM)
 
 
-def pairing(size):
-    if size & (size - 1) == 0:
-        return (lambda i, k: i ^ k), (lambda i, k: i ^ k)
-    return (lambda i, k: (i + k) % size), (lambda i, k: (i + size - k) % size)
-
-
-def exchange(pieces, axis, size):
-    to, _ = pairing(size)
+def offsets(size):
+    if size & (size - 1):
+        return [[(i + k) % size for i in range(size)] for k in range(1, size)]
+    return [[i ^ k for i in range(size)] for k in range(1, size)]
+
+
+def rounds(size):
+    if size == 4:
+        return [[2, 0, 3, 1], [3, 2, 1, 0], [1, 3, 0, 2]]
+    return offsets(size)
+
+
+def pick(table, at):
+    value = table[0]
+    for i in range(1, len(table)):
+        value = jnp.where(at == i, table[i], value)
+    return value
+
+
+def send(pieces, axis, permutations):
     return [
-        lax.ppermute(pieces[k - 1], axis, [(i, to(i, k)) for i in range(size)])
-        for k in range(size - 1, 0, -1)
-    ][::-1]
+        lax.ppermute(piece, axis, list(enumerate(target)))
+        for piece, target in zip(pieces, permutations)
+    ]
 
 
 def gather_pairs(part, axis, size):
     if size & (size - 1):
-        return exchange([part] * (size - 1), axis, size)
+        return send([part] * (size - 1), axis, offsets(size))
     swap = [(i, i ^ 1) for i in range(size)]
     far = [lax.ppermute(part, axis, [(i, i ^ k) for i in range(size)]) for k in range(2, size, 2)]
     near = [lax.ppermute(a, axis, swap) for a in [part] + far]
@@ -60,10 +72,14 @@
     return (lax.axis_index("row") == lax.axis_index("col")).astype(jnp.float32)
 
 
-def stage_kernel(values, tiles, sem):
-    copy = pltpu.make_async_copy(values, tiles, sem)
-    copy.start()
-    copy.wait()
+def stage_kernel(values, tiles, sems):
+    copies = [
+        pltpu.make_async_copy(values.at[s], tiles.at[s], sems.at[s]) for s in range(tiles.shape[0])
+    ]
+    for copy in copies:
+        copy.start()
+    for copy in copies:
+        copy.wait()
 
 
 def turn_kernel(tiles, turned):
@@ -73,11 +89,11 @@
 
 def first_kernel(size, *refs):
     pieces, (tiles, rows, cols, count, mobility, out, whole, total) = refs[:size], refs[size:]
-    _, source_of = pairing(size)
     me = lax.axis_index("col")
     piece, group_len = pieces[0].shape[1], whole.shape[1]
-    for k in range(size):
-        whole[:, lanes(source_of(me, k) * piece, piece)] = pieces[k][...]
+    sources = [me] + [pick([target.index(i) for i in range(size)], me) for target in rounds(size)]
+    for source, arrived in zip(sources, pieces):
+        whole[:, lanes(source * piece, piece)] = arrived[...]
     total[:, :group_len] = self_factor() * (mobility[...] - SHIFT) * whole[...].astype(jnp.float32)
     add_slots(whole, total, tiles, rows, cols, count)
     out[...] = total[:, :group_len].astype(out.dtype)
@@ -96,11 +112,10 @@
     first[...] = whole[:, lanes(lax.axis_index("row") * row_piece, row_piece)]
     total[:, :group_len] = self_factor() * (mobility[...] - SHIFT) * whole[...].astype(jnp.float32)
     add_slots(whole, total, tiles, cols, rows, count)
-    to, _ = pairing(n_col)
     me = lax.axis_index("col")
     piece = outs[0].shape[1]
-    for k in range(n_col):
-        outs[k][...] = total[:, lanes(to(me, k) * piece, piece)].astype(outs[k].dtype)
+    for target, out in zip([me] + [pick(p, me) for p in offsets(n_col)], outs):
+        out[...] = total[:, lanes(target * piece, piece)].astype(out.dtype)
 
 
 def last_kernel(size, *refs):
@@ -127,13 +142,13 @@
         pltpu.VMEM((vectors, group_len + span), jnp.float32),
     ]
     params = pltpu.CompilerParams(vmem_limit_bytes=VMEM_LIMIT)
-    arrived = exchange([own] * (n_col - 1), "col", n_col)
+    arrived = send([own] * (n_col - 1), "col", rounds(n_col))
     staged = pl.pallas_call(
         stage_kernel,
         out_shape=jax.ShapeDtypeStruct(tiles.shape, tiles.dtype),
         in_specs=[HBM],
         out_specs=VMEM,
-        scratch_shapes=[pltpu.SemaphoreType.DMA],
+        scratch_shapes=[pltpu.SemaphoreType.DMA((slots,))],
         compiler_params=pltpu.CompilerParams(vmem_limit_bytes=STAGE_LIMIT),
         cost_estimate=pl.CostEstimate(flops=0, transcendentals=0, bytes_accessed=4 * tiles.size),
         name="stage",
@@ -169,7 +184,7 @@
         compiler_params=params,
         name="second_product",
     )(*parts, turned, *tables[1:])
-    arrived = [seconds[0]] + exchange(seconds[1:], "col", n_col)
+    arrived = [seconds[0]] + send(seconds[1:], "col", offsets(n_col))
     first, second = pl.pallas_call(
         functools.partial(last_kernel, n_col),
         out_shape=[row_type, piece_type],

time: 25.4 us -> 24.9 us (0.980)
  waiting for transfers between devices: 8 us -> 6.11 us
  starting transfers between devices: 11.8 us -> 13.1 us
    ppermute x6, waiting for transfers between devices: 4.25 us -> 2.36 us  [send(): lax.ppermute(piece, axis, list(enumerate(target)))]
    ppermute x6, starting transfers between devices: 10.2 us -> 11.6 us  [send(): lax.ppermute(piece, axis, list(enumerate(target)))]
where the time goes in v5:
time: 24.9 us; the launch traced here: 24.7 us
  starting transfers between devices  13.1 us (53%)
  waiting for transfers between devices  6.11 us (25%)
  Pallas kernels  4.05 us (16%)
  between operations  1.39 us (6%)
    ppermute x6, starting transfers between devices, send(): lax.ppermute(piece, axis, list(enumerate(target)))  11.6 us
    ppermute x1, waiting for transfers between devices, gather_pairs(): lax.ppermute(part, axis, [(i, i ^ k) for i in range(size)])  3.12 us
    ppermute x6, waiting for transfers between devices, send(): lax.ppermute(piece, axis, list(enumerate(target)))  2.36 us
    pallas_call x1, Pallas kernels, on_device(): pl.pallas_call(stage_kernel, out_shape=jax.ShapeDtypeStruct(tiles.shape,...  1.68 us
    ppermute x1, starting transfers between devices, gather_pairs(): lax.ppermute(part, axis, [(i, i ^ k) for i in range(size)])  1.56 us
    pallas_call x1, Pallas kernels, on_device(): pl.pallas_call(turn_kernel, out_shape=jax.ShapeDtypeStruct(tiles.shape, t...  0.65 us
    pallas_call x1, Pallas kernels, on_device(): pl.pallas_call(functools.partial(last_kernel, n_col), out_shape=[row_type...  0.63 us
    ppermute x2, waiting for transfers between devices, gather_pairs(): near = [lax.ppermute(a, axis, swap) for a in [part] + far]  0.63 us
  transfers between devices with their start and end apart: 9, of which 5 were waited for; matrix products, arithmetic and copies ran while one was open for 0% of the time, Pallas kernels for 9%

profile of v5, /device:TPU:0, one launch (start us, length us, event | category | flops | bytes accessed | tf_op | source)
XLA Modules:
  0.0 24.7 jit_solution(2312366577557865739)
XLA Ops:
  0.6 3.1 %collective-permute-start.2 = (bf16[8,1536]{1,0:T(8,128)(2,1)}, bf16[8,1536]{1,0:T(8,128)(2,1)S(1)}, u32[]{:S(2)}, u32[]{:S(2)}) collective-permute-start(bf16[8,1536]{1,0:T(8,128)(2,1)} %bitcast.4), channel_id=1, source_target_pairs={{0,1},{1,3},{2,0},{3,2},{4,5},{5,7},{6,4},{7,6},{8,9},{9,11},{10,8... | collective-permute-start | bytes 73736 | tf_op jit(solution)/shard_map/ppermute | solution.py:40
  3.7 2.5 %collective-permute-start.1 = (bf16[8,1536]{1,0:T(8,128)(2,1)}, bf16[8,1536]{1,0:T(8,128)(2,1)S(1)}, u32[]{:S(2)}, u32[]{:S(2)}) collective-permute-start(bf16[8,1536]{1,0:T(8,128)(2,1)} %bitcast.5), channel_id=1, source_target_pairs={{0,3},{1,2},{2,1},{3,0},{4,7},{5,6},{6,5},{7,4},{8,11},{9,10},{10,... | collective-permute-start | bytes 73736 | tf_op jit(solution)/shard_map/ppermute | solution.py:40
  6.2 1.6 %collective-permute-start = (bf16[8,1536]{1,0:T(8,128)(2,1)}, bf16[8,1536]{1,0:T(8,128)(2,1)S(1)}, u32[]{:S(2)}, u32[]{:S(2)}) collective-permute-start(bf16[8,1536]{1,0:T(8,128)(2,1)} %bitcast.6), channel_id=1, source_target_pairs={{0,2},{1,0},{2,3},{3,1},{4,6},{5,4},{6,7},{7,5},{8,10},{9,8},{10,1... | collective-permute-start | bytes 73736 | tf_op jit(solution)/shard_map/ppermute | solution.py:40
  8.4 0.0 copy-start
  8.4 0.0 copy-start.1
  8.4 0.0 copy-start.2
  8.4 0.0 copy-start.3
  8.5 1.7 %stage.1.refs_4_.tiles = bf16[8,384,384]{2,1,0:T(8,128)(2,1)S(1)} custom-call(bf16[8,384,384]{2,1,0:T(8,128)(2,1)} %bitcast.9), custom_call_target="tpu_custom_call" | custom-call | bytes 4718592 | tf_op jit(solution)/shard_map/stage/pallas_call | solution.py:146
  10.1 0.0 collective-permute-done.2.refs_3_
  10.1 0.0 collective-permute-done.1.refs_2_
  10.2 0.1 collective-permute-done.refs_1_
  10.2 0.0 copy-done
  10.2 0.0 copy-done.1
  10.2 0.0 copy-done.2
  10.2 0.0 copy-done.3
  10.2 0.5 %first_product.1.refs_0_ = bf16[8,6144]{1,0:T(8,128)(2,1)S(1)} custom-call(bf16[8,1536]{1,0:T(8,128)(2,1)S(1)} %bitcast.7, bf16[8,1536]{1,0:T(8,128)(2,1)S(1)} %collective-permute-done.refs_1_, bf16[8,1536]{1,0:T(8,128)(2,1)S(1)} %collective-permute-done.1.refs_2_, bf16[8,1536]{1,0:T(8,128)(2,1)S(1)} %collective-permute-done.2.refs_3_, ...), custom_call_target="tpu_custom_call" | custom-call | tf_op jit(solution)/shard_map/first_product/pallas_call | solution.py:168
  10.8 1.6 %collective-permute-start.4 = (bf16[8,6144]{1,0:T(8,128)(2,1)S(1)}, bf16[8,6144]{1,0:T(8,128)(2,1)S(1)}, u32[]{:S(2)}, u32[]{:S(2)}) collective-permute-start(bf16[8,6144]{1,0:T(8,128)(2,1)S(1)} %first_product.1.refs_0_), channel_id=1, source_target_pairs={{0,8},{4,12},{8,0},{12,4},{1,9},{5,13},{9,1},{13,5},{2,10},{6,14},... | collective-permute-start | bytes 294920 | tf_op jit(solution)/shard_map/ppermute | solution.py:49
  12.3 0.0 collective-permute-start.3
  12.3 3.1 %collective-permute-done.4.refs_3_ = bf16[8,6144]{1,0:T(8,128)(2,1)S(1)} collective-permute-done((bf16[8,6144]{1,0:T(8,128)(2,1)S(1)}, bf16[8,6144]{1,0:T(8,128)(2,1)S(1)}, u32[]{:S(2)}, u32[]{:S(2)}) %collective-permute-start.4) | collective-permute-done | bytes 98336 | tf_op jit(solution)/shard_map/ppermute | solution.py:49
  15.5 0.0 collective-permute-start.5
  15.5 0.7 %turn.1.refs_4_ = bf16[8,384,384]{2,1,0:T(8,128)(2,1)S(1)} custom-call(bf16[8,384,384]{2,1,0:T(8,128)(2,1)S(1)} %stage.1.refs_4_.tiles), custom_call_target="tpu_custom_call" | custom-call | bytes 4718592 | tf_op jit(solution)/shard_map/turn/pallas_call | solution.py:156
  16.1 0.0 collective-permute-done.3.refs_1_
  16.1 0.6 %collective-permute-done.5.refs_2_ = bf16[8,6144]{1,0:T(8,128)(2,1)S(1)} collective-permute-done((bf16[8,6144]{1,0:T(8,128)(2,1)S(1)}, bf16[8,6144]{1,0:T(8,128)(2,1)S(1)}, u32[]{:S(2)}, u32[]{:S(2)}) %collective-permute-start.5) | collective-permute-done | bytes 98336 | tf_op jit(solution)/shard_map/ppermute | solution.py:50
  16.8 0.6 %second_product.1 = (bf16[8,1536]{1,0:T(8,128)(2,1)S(1)}, bf16[8,1536]{1,0:T(8,128)(2,1)S(1)}, bf16[8,1536]{1,0:T(8,128)(2,1)S(1)}, bf16[8,1536]{1,0:T(8,128)(2,1)S(1)}, bf16[8,1536]{1,0:T(8,128)(2,1)S(1)}) custom-call(bf16[8,6144]{1,0:T(8,128)(2,1)S(1)} %first_product.1.refs_0_, bf16[8,6144]{1,0:T(8,128)(2,1)S(1)} %collective-permute-done.3.refs_1_, ...), custom_call_target="tpu_custom_call" | custom-call | tf_op jit(solution)/shard_map/second_product/pallas_call | solution.py:178
  17.3 2.0 %collective-permute-start.6 = (bf16[8,1536]{1,0:T(8,128)(2,1)S(1)}, bf16[8,1536]{1,0:T(8,128)(2,1)S(1)}, u32[]{:S(2)}, u32[]{:S(2)}) collective-permute-start(bf16[8,1536]{1,0:T(8,128)(2,1)S(1)} %get-tuple-element.9), channel_id=1, source_target_pairs={{0,3},{1,2},{2,1},{3,0},{4,7},{5,6},{6,5},{7,4},{8,11},{9,10},{10,... | collective-permute-start | bytes 73736 | tf_op jit(solution)/shard_map/ppermute | solution.py:40
  19.3 0.6 %collective-permute-start.7 = (bf16[8,1536]{1,0:T(8,128)(2,1)S(1)}, bf16[8,1536]{1,0:T(8,128)(2,1)S(1)}, u32[]{:S(2)}, u32[]{:S(2)}) collective-permute-start(bf16[8,1536]{1,0:T(8,128)(2,1)S(1)} %get-tuple-element.10), channel_id=1, source_target_pairs={{0,2},{1,3},{2,0},{3,1},{4,6},{5,7},{6,4},{7,5},{8,10},{9,11},{10,... | collective-permute-start | bytes 73736 | tf_op jit(solution)/shard_map/ppermute | solution.py:40
  19.9 1.8 %collective-permute-start.8 = (bf16[8,1536]{1,0:T(8,128)(2,1)S(1)}, bf16[8,1536]{1,0:T(8,128)(2,1)S(1)}, u32[]{:S(2)}, u32[]{:S(2)}) collective-permute-start(bf16[8,1536]{1,0:T(8,128)(2,1)S(1)} %get-tuple-element.11), channel_id=1, source_target_pairs={{0,1},{1,0},{2,3},{3,2},{4,5},{5,4},{6,7},{7,6},{8,9},{9,8},{10,11... | collective-permute-start | bytes 73736 | tf_op jit(solution)/shard_map/ppermute | solution.py:40
  21.8 1.3 %collective-permute-done.6.refs_0_ = bf16[8,1536]{1,0:T(8,128)(2,1)S(1)} collective-permute-done((bf16[8,1536]{1,0:T(8,128)(2,1)S(1)}, bf16[8,1536]{1,0:T(8,128)(2,1)S(1)}, u32[]{:S(2)}, u32[]{:S(2)}) %collective-permute-start.6) | collective-permute-done | bytes 24608 | tf_op jit(solution)/shard_map/ppermute | solution.py:40
  23.1 0.9 %collective-permute-done.7.refs_1_ = bf16[8,1536]{1,0:T(8,128)(2,1)S(1)} collective-permute-done((bf16[8,1536]{1,0:T(8,128)(2,1)S(1)}, bf16[8,1536]{1,0:T(8,128)(2,1)S(1)}, u32[]{:S(2)}, u32[]{:S(2)}) %collective-permute-start.7) | collective-permute-done | bytes 24608 | tf_op jit(solution)/shard_map/ppermute | solution.py:40
  24.1 0.0 collective-permute-done.8.refs_2_
  24.1 0.6 %second_term.1 = (bf16[8,1536]{1,0:T(8,128)(2,1)}, bf16[8,1536]{1,0:T(8,128)(2,1)}) custom-call(bf16[8,1536]{1,0:T(8,128)(2,1)S(1)} %collective-permute-done.6.refs_0_, bf16[8,1536]{1,0:T(8,128)(2,1)S(1)} %collective-permute-done.7.refs_1_, bf16[8,1536]{1,0:T(8,128)(2,1)S(1)} %collective-permute-done.8.refs_2_, ...), custom_call_target="tpu_custom_call" | custom-call | tf_op jit(solution)/shard_map/second_term/pallas_call | solution.py:188
Async XLA Ops:
  0.6 9.5 %collective-permute-start.2 = (bf16[8,1536]{1,0:T(8,128)(2,1)}, bf16[8,1536]{1,0:T(8,128)(2,1)S(1)}, u32[]{:S(2)}, u32[]{:S(2)}) collective-permute-start(bf16[8,1536]{1,0:T(8,128)(2,1)} %bitcast.4), channel_id=1, source_target_pairs={{0,1},{1,3},{2,0},{3,2},{4,5},{5,7},{6,4},{7,6},{8,9},{9,11},{10,8... | collective-permute-start | bytes 73736 | tf_op jit(solution)/shard_map/ppermute | solution.py:40
  3.7 6.4 %collective-permute-start.1 = (bf16[8,1536]{1,0:T(8,128)(2,1)}, bf16[8,1536]{1,0:T(8,128)(2,1)S(1)}, u32[]{:S(2)}, u32[]{:S(2)}) collective-permute-start(bf16[8,1536]{1,0:T(8,128)(2,1)} %bitcast.5), channel_id=1, source_target_pairs={{0,3},{1,2},{2,1},{3,0},{4,7},{5,6},{6,5},{7,4},{8,11},{9,10},{10,... | collective-permute-start | bytes 73736 | tf_op jit(solution)/shard_map/ppermute | solution.py:40
  6.2 4.0 %collective-permute-start = (bf16[8,1536]{1,0:T(8,128)(2,1)}, bf16[8,1536]{1,0:T(8,128)(2,1)S(1)}, u32[]{:S(2)}, u32[]{:S(2)}) collective-permute-start(bf16[8,1536]{1,0:T(8,128)(2,1)} %bitcast.6), channel_id=1, source_target_pairs={{0,2},{1,0},{2,3},{3,1},{4,6},{5,4},{6,7},{7,5},{8,10},{9,8},{10,1... | collective-permute-start | bytes 73736 | tf_op jit(solution)/shard_map/ppermute | solution.py:40
  8.4 1.8 %copy-start = (f32[1,6144]{1,0:T(1,128)S(1)}, f32[1,6144]{1,0:T(1,128)}, u32[]{:S(2)}) copy-start(f32[1,6144]{1,0:T(1,128)} %refs_8_.3) | copy-start | bytes 73732
  8.4 1.8 %copy-start.1 = (bf16[8,1,1,1536]{3,0,2,1:T(8,128)(2,1)S(1)}, bf16[8,1,1,1536]{3,0,2,1:T(8,128)(2,1)}, u32[]{:S(2)}) copy-start(bf16[8,1,1,1536]{3,0,2,1:T(8,128)(2,1)} %param.6) | copy-start | bytes 73732
  8.4 1.8 %copy-start.2 = (s32[1,1,8]{2,1,0:T(1,128)S(1)}, s32[1,1,8]{2,1,0:T(1,128)}, u32[]{:S(2)}) copy-start(s32[1,1,8]{2,1,0:T(1,128)} %refs_5_.3) | copy-start | bytes 100
  8.4 1.8 %copy-start.3 = (s32[1,1,8]{2,1,0:T(1,128)S(1)}, s32[1,1,8]{2,1,0:T(1,128)}, u32[]{:S(2)}) copy-start(s32[1,1,8]{2,1,0:T(1,128)} %refs_6_.3) | copy-start | bytes 100
  10.8 4.7 %collective-permute-start.4 = (bf16[8,6144]{1,0:T(8,128)(2,1)S(1)}, bf16[8,6144]{1,0:T(8,128)(2,1)S(1)}, u32[]{:S(2)}, u32[]{:S(2)}) collective-permute-start(bf16[8,6144]{1,0:T(8,128)(2,1)S(1)} %first_product.1.refs_0_), channel_id=1, source_target_pairs={{0,8},{4,12},{8,0},{12,4},{1,9},{5,13},{9,1},{13,5},{2,10},{6,14},... | collective-permute-start | bytes 294920 | tf_op jit(solution)/shard_map/ppermute | solution.py:49
  12.3 3.8 %collective-permute-start.3 = (bf16[8,6144]{1,0:T(8,128)(2,1)S(1)}, bf16[8,6144]{1,0:T(8,128)(2,1)S(1)}, u32[]{:S(2)}, u32[]{:S(2)}) collective-permute-start(bf16[8,6144]{1,0:T(8,128)(2,1)S(1)} %first_product.1.refs_0_), channel_id=1, source_target_pairs={{0,4},{4,0},{8,12},{12,8},{1,5},{5,1},{9,13},{13,9},{2,6},{6,2},{1... | collective-permute-start | bytes 294920 | tf_op jit(solution)/shard_map/ppermute | solution.py:50
  15.5 1.3 %collective-permute-start.5 = (bf16[8,6144]{1,0:T(8,128)(2,1)S(1)}, bf16[8,6144]{1,0:T(8,128)(2,1)S(1)}, u32[]{:S(2)}, u32[]{:S(2)}) collective-permute-start(bf16[8,6144]{1,0:T(8,128)(2,1)S(1)} %collective-permute-done.4.refs_3_), channel_id=1, source_target_pairs={{0,4},{4,0},{8,12},{12,8},{1,5},{5,1},{9,13},{13,9},{2,6},{6,2},{1... | collective-permute-start | bytes 294920 | tf_op jit(solution)/shard_map/ppermute | solution.py:50
  17.3 5.8 %collective-permute-start.6 = (bf16[8,1536]{1,0:T(8,128)(2,1)S(1)}, bf16[8,1536]{1,0:T(8,128)(2,1)S(1)}, u32[]{:S(2)}, u32[]{:S(2)}) collective-permute-start(bf16[8,1536]{1,0:T(8,128)(2,1)S(1)} %get-tuple-element.9), channel_id=1, source_target_pairs={{0,3},{1,2},{2,1},{3,0},{4,7},{5,6},{6,5},{7,4},{8,11},{9,10},{10,... | collective-permute-start | bytes 73736 | tf_op jit(solution)/shard_map/ppermute | solution.py:40
  19.3 4.7 %collective-permute-start.7 = (bf16[8,1536]{1,0:T(8,128)(2,1)S(1)}, bf16[8,1536]{1,0:T(8,128)(2,1)S(1)}, u32[]{:S(2)}, u32[]{:S(2)}) collective-permute-start(bf16[8,1536]{1,0:T(8,128)(2,1)S(1)} %get-tuple-element.10), channel_id=1, source_target_pairs={{0,2},{1,3},{2,0},{3,1},{4,6},{5,7},{6,4},{7,5},{8,10},{9,11},{10,... | collective-permute-start | bytes 73736 | tf_op jit(solution)/shard_map/ppermute | solution.py:40
  19.9 4.1 %collective-permute-start.8 = (bf16[8,1536]{1,0:T(8,128)(2,1)S(1)}, bf16[8,1536]{1,0:T(8,128)(2,1)S(1)}, u32[]{:S(2)}, u32[]{:S(2)}) collective-permute-start(bf16[8,1536]{1,0:T(8,128)(2,1)S(1)} %get-tuple-element.11), channel_id=1, source_target_pairs={{0,1},{1,0},{2,3},{3,2},{4,5},{5,4},{6,7},{7,6},{8,9},{9,8},{10,11... | collective-permute-start | bytes 73736 | tf_op jit(solution)/shard_map/ppermute | solution.py:40

commit v6 on v5

--- a/solution.py
+++ b/solution.py
@@ -24,7 +24,7 @@
 
 def rounds(size):
     if size == 4:
-        return [[2, 0, 3, 1], [3, 2, 1, 0], [1, 3, 0, 2]]
+        return [[1, 3, 0, 2], [3, 2, 1, 0], [2, 0, 3, 1]]
     return offsets(size)
 
 
@@ -44,11 +44,11 @@
 
 def gather_pairs(part, axis, size):
     if size & (size - 1):
-        return send([part] * (size - 1), axis, offsets(size))
+        return [part], send([part] * (size - 1), axis, offsets(size))
     swap = [(i, i ^ 1) for i in range(size)]
     far = [lax.ppermute(part, axis, [(i, i ^ k) for i in range(size)]) for k in range(2, size, 2)]
     near = [lax.ppermute(a, axis, swap) for a in [part] + far]
-    return near + far
+    return [part, near[0], *far], near[1:]
 
 
 def lanes(start, length):
@@ -82,7 +82,16 @@
         copy.wait()
 
 
-def turn_kernel(tiles, turned):
+def added(parts):
+    sums = parts[0][...].astype(jnp.float32)
+    for part in parts[1:]:
+        sums = sums + part[...].astype(jnp.float32)
+    return sums
+
+
+def turn_kernel(tiles, *refs):
+    parts, (turned, sums) = refs[:-2], refs[-2:]
+    sums[...] = added(parts)
     for s in range(tiles.shape[0]):
         turned[s] = tiles[s].T
 
@@ -99,15 +108,12 @@
     out[...] = total[:, :group_len].astype(out.dtype)
 
 
-def second_kernel(n_row, n_col, *refs):
-    parts, rest = refs[:n_row], refs[n_row + 5 :]
-    tiles, rows, cols, count, mobility = refs[n_row : n_row + 5]
+def second_kernel(n_parts, n_col, *refs):
+    parts, rest = refs[:n_parts], refs[n_parts + 5 :]
+    tiles, rows, cols, count, mobility = refs[n_parts : n_parts + 5]
     first, outs, (whole, total) = rest[0], rest[1 : 1 + n_col], rest[1 + n_col :]
     group_len = whole.shape[1]
-    sums = parts[0][...].astype(jnp.float32)
-    for part in parts[1:]:
-        sums = sums + part[...].astype(jnp.float32)
-    whole[...] = (sums * (1.0 / HALF_WIDTH)).astype(whole.dtype)
+    whole[...] = (added(parts) * (1.0 / HALF_WIDTH)).astype(whole.dtype)
     row_piece = first.shape[1]
     first[...] = whole[:, lanes(lax.axis_index("row") * row_piece, row_piece)]
     total[:, :group_len] = self_factor() * (mobility[...] - SHIFT) * whole[...].astype(jnp.float32)
@@ -121,10 +127,7 @@
 def last_kernel(size, *refs):
     parts, (noise, first, first_out, out) = refs[:size], refs[size:]
     first_out[...] = first[...]
-    sums = parts[0][...].astype(jnp.float32)
-    for part in parts[1:]:
-        sums = sums + part[...].astype(jnp.float32)
-    out[...] = ((2.0 / HALF_WIDTH) * sums - noise[...].astype(jnp.float32)).astype(out.dtype)
+    out[...] = ((2.0 / HALF_WIDTH) * added(parts) - noise[...].astype(jnp.float32)).astype(out.dtype)
 
 
 def on_device(noise, block_values, block_rows, block_cols, block_count, self_mobility):
@@ -153,15 +156,6 @@
         cost_estimate=pl.CostEstimate(flops=0, transcendentals=0, bytes_accessed=4 * tiles.size),
         name="stage",
     )(tiles)
-    turned = pl.pallas_call(
-        turn_kernel,
-        out_shape=jax.ShapeDtypeStruct(tiles.shape, tiles.dtype),
-        in_specs=[VMEM],
-        out_specs=VMEM,
-        compiler_params=params,
-        cost_estimate=pl.CostEstimate(flops=0, transcendentals=0, bytes_accessed=4 * tiles.size),
-        name="turn",
-    )(staged)
     tables = (staged, block_rows, block_cols, block_count, self_mobility)
     table_specs = [VMEM, VMEM, VMEM, VMEM, VMEM]
     pieces = [own] + arrived
@@ -174,11 +168,24 @@
         compiler_params=params,
         name="first_product",
     )(*pieces, *tables)
-    parts = [part] + gather_pairs(part, "row", n_row)
+    here, late = gather_pairs(part, "row", n_row)
+    turned, summed = pl.pallas_call(
+        turn_kernel,
+        out_shape=[
+            jax.ShapeDtypeStruct(tiles.shape, tiles.dtype),
+            jax.ShapeDtypeStruct((vectors, group_len), jnp.float32),
+        ],
+        in_specs=[VMEM] * (1 + len(here)),
+        out_specs=[VMEM] * 2,
+        compiler_params=params,
+        cost_estimate=pl.CostEstimate(flops=0, transcendentals=0, bytes_accessed=4 * tiles.size),
+        name="turn",
+    )(staged, *here)
+    parts = [summed, *late]
     first, *seconds = pl.pallas_call(
-        functools.partial(second_kernel, n_row, n_col),
+        functools.partial(second_kernel, len(parts), n_col),
         out_shape=[row_type] + [piece_type] * n_col,
-        in_specs=[VMEM] * n_row + table_specs,
+        in_specs=[VMEM] * len(parts) + table_specs,
         out_specs=[VMEM] * (1 + n_col),
         scratch_shapes=scratch,
         compiler_params=params,

time: 24.9 us -> 24.8 us (level)
  transfers between devices with their start and end apart: 9 -> 9, of which waited for: 5 -> 5; matrix products, arithmetic and copies ran while one was open for 0% -> 0% of each run, Pallas kernels for 9% -> 10%
where the time goes in v6:
time: 24.8 us; the launch traced here: 24.7 us
  starting transfers between devices  13.1 us (53%)
  waiting for transfers between devices  6.11 us (25%)
  Pallas kernels  4.05 us (16%)
  between operations  1.35 us (5%)
    ppermute x6, starting transfers between devices, send(): lax.ppermute(piece, axis, list(enumerate(target)))  11.6 us
    ppermute x1, waiting for transfers between devices, gather_pairs(): lax.ppermute(part, axis, [(i, i ^ k) for i in range(size)])  3.12 us
    ppermute x6, waiting for transfers between devices, send(): lax.ppermute(piece, axis, list(enumerate(target)))  2.37 us
    pallas_call x1, Pallas kernels, on_device(): pl.pallas_call(stage_kernel, out_shape=jax.ShapeDtypeStruct(tiles.shape,...  1.7 us
    ppermute x1, starting transfers between devices, gather_pairs(): lax.ppermute(part, axis, [(i, i ^ k) for i in range(size)])  1.56 us
    pallas_call x1, Pallas kernels, on_device(): pl.pallas_call(turn_kernel, out_shape=[jax.ShapeDtypeStruct(tiles.shape,...  0.67 us
    pallas_call x1, Pallas kernels, on_device(): pl.pallas_call(functools.partial(last_kernel, n_col), out_shape=[row_type...  0.63 us
    ppermute x2, waiting for transfers between devices, gather_pairs(): near = [lax.ppermute(a, axis, swap) for a in [part] + far]  0.62 us
  transfers between devices with their start and end apart: 9, of which 5 were waited for; matrix products, arithmetic and copies ran while one was open for 0% of the time, Pallas kernels for 10%

profile of v6, /device:TPU:0, one launch (start us, length us, event | category | flops | bytes accessed | tf_op | source)
XLA Modules:
  0.0 24.7 jit_solution(14403402186743701981)
XLA Ops:
  0.6 3.1 %collective-permute-start = (bf16[8,1536]{1,0:T(8,128)(2,1)}, bf16[8,1536]{1,0:T(8,128)(2,1)S(1)}, u32[]{:S(2)}, u32[]{:S(2)}) collective-permute-start(bf16[8,1536]{1,0:T(8,128)(2,1)} %bitcast.4), channel_id=1, source_target_pairs={{0,1},{1,3},{2,0},{3,2},{4,5},{5,7},{6,4},{7,6},{8,9},{9,11},{10,8... | collective-permute-start | bytes 73736 | tf_op jit(solution)/shard_map/ppermute | solution.py:40
  3.7 2.5 %collective-permute-start.1 = (bf16[8,1536]{1,0:T(8,128)(2,1)}, bf16[8,1536]{1,0:T(8,128)(2,1)S(1)}, u32[]{:S(2)}, u32[]{:S(2)}) collective-permute-start(bf16[8,1536]{1,0:T(8,128)(2,1)} %bitcast.5), channel_id=1, source_target_pairs={{0,3},{1,2},{2,1},{3,0},{4,7},{5,6},{6,5},{7,4},{8,11},{9,10},{10,... | collective-permute-start | bytes 73736 | tf_op jit(solution)/shard_map/ppermute | solution.py:40
  6.2 1.6 %collective-permute-start.2 = (bf16[8,1536]{1,0:T(8,128)(2,1)}, bf16[8,1536]{1,0:T(8,128)(2,1)S(1)}, u32[]{:S(2)}, u32[]{:S(2)}) collective-permute-start(bf16[8,1536]{1,0:T(8,128)(2,1)} %bitcast.6), channel_id=1, source_target_pairs={{0,2},{1,0},{2,3},{3,1},{4,6},{5,4},{6,7},{7,5},{8,10},{9,8},{10,1... | collective-permute-start | bytes 73736 | tf_op jit(solution)/shard_map/ppermute | solution.py:40
  7.8 0.0 copy-start
  7.8 0.0 copy-start.1
  7.8 0.0 copy-start.2
  7.8 0.0 copy-start.3
  7.8 1.7 %stage.1.refs_4_.tiles = bf16[8,384,384]{2,1,0:T(8,128)(2,1)S(1)} custom-call(bf16[8,384,384]{2,1,0:T(8,128)(2,1)} %bitcast.9), custom_call_target="tpu_custom_call" | custom-call | bytes 4718592 | tf_op jit(solution)/shard_map/stage/pallas_call | solution.py:149
  10.1 0.0 collective-permute-done.refs_1_
  10.1 0.0 collective-permute-done.1.refs_2_
  10.2 0.1 collective-permute-done.2.refs_3_
  10.2 0.0 copy-done
  10.2 0.0 copy-done.1
  10.2 0.0 copy-done.2
  10.2 0.0 copy-done.3
  10.2 0.5 %first_product.1.refs_0_ = bf16[8,6144]{1,0:T(8,128)(2,1)S(1)} custom-call(bf16[8,1536]{1,0:T(8,128)(2,1)S(1)} %bitcast.7, bf16[8,1536]{1,0:T(8,128)(2,1)S(1)} %collective-permute-done.refs_1_, bf16[8,1536]{1,0:T(8,128)(2,1)S(1)} %collective-permute-done.1.refs_2_, bf16[8,1536]{1,0:T(8,128)(2,1)S(1)} %collective-permute-done.2.refs_3_, ...), custom_call_target="tpu_custom_call" | custom-call | tf_op jit(solution)/shard_map/first_product/pallas_call | solution.py:162
  10.8 1.6 %collective-permute-start.4 = (bf16[8,6144]{1,0:T(8,128)(2,1)S(1)}, bf16[8,6144]{1,0:T(8,128)(2,1)S(1)}, u32[]{:S(2)}, u32[]{:S(2)}) collective-permute-start(bf16[8,6144]{1,0:T(8,128)(2,1)S(1)} %first_product.1.refs_0_), channel_id=1, source_target_pairs={{0,8},{4,12},{8,0},{12,4},{1,9},{5,13},{9,1},{13,5},{2,10},{6,14},... | collective-permute-start | bytes 294920 | tf_op jit(solution)/shard_map/ppermute | solution.py:49
  12.3 0.0 collective-permute-start.3
  12.3 3.1 %collective-permute-done.4.refs_2_ = bf16[8,6144]{1,0:T(8,128)(2,1)S(1)} collective-permute-done((bf16[8,6144]{1,0:T(8,128)(2,1)S(1)}, bf16[8,6144]{1,0:T(8,128)(2,1)S(1)}, u32[]{:S(2)}, u32[]{:S(2)}) %collective-permute-start.4) | collective-permute-done | bytes 98336 | tf_op jit(solution)/shard_map/ppermute | solution.py:49
  15.4 0.0 collective-permute-start.5
  15.5 0.0 collective-permute-done.3.refs_1_
  15.5 0.7 %turn.1 = (bf16[8,384,384]{2,1,0:T(8,128)(2,1)S(1)}, f32[8,6144]{1,0:T(8,128)S(1)}) custom-call(bf16[8,384,384]{2,1,0:T(8,128)(2,1)S(1)} %stage.1.refs_4_.tiles, bf16[8,6144]{1,0:T(8,128)(2,1)S(1)} %first_product.1.refs_0_, bf16[8,6144]{1,0:T(8,128)(2,1)S(1)} %collective-permute-done.3.refs_1_, bf16[8,6144]{1,0:T(8,128)(2,1)S(1)} %collective-permute-done.4.refs_2_), custom_call_target="tpu_custom_call" | custom-call | bytes 4718592 | tf_op jit(solution)/shard_map/turn/pallas_call | solution.py:172
  16.1 0.6 %collective-permute-done.5.refs_1_ = bf16[8,6144]{1,0:T(8,128)(2,1)S(1)} collective-permute-done((bf16[8,6144]{1,0:T(8,128)(2,1)S(1)}, bf16[8,6144]{1,0:T(8,128)(2,1)S(1)}, u32[]{:S(2)}, u32[]{:S(2)}) %collective-permute-start.5) | collective-permute-done | bytes 98336 | tf_op jit(solution)/shard_map/ppermute | solution.py:50
  16.8 0.5 %second_product.1 = (bf16[8,1536]{1,0:T(8,128)(2,1)S(1)}, bf16[8,1536]{1,0:T(8,128)(2,1)S(1)}, bf16[8,1536]{1,0:T(8,128)(2,1)S(1)}, bf16[8,1536]{1,0:T(8,128)(2,1)S(1)}, bf16[8,1536]{1,0:T(8,128)(2,1)S(1)}) custom-call(f32[8,6144]{1,0:T(8,128)S(1)} %get-tuple-element.11.refs_0_, bf16[8,6144]{1,0:T(8,128)(2,1)S(1)} %collective-permute-done.5.refs_1_, ...), custom_call_target="tpu_custom_call" | custom-call | tf_op jit(solution)/shard_map/second_product/pallas_call | solution.py:185
  17.3 2.0 %collective-permute-start.6 = (bf16[8,1536]{1,0:T(8,128)(2,1)S(1)}, bf16[8,1536]{1,0:T(8,128)(2,1)S(1)}, u32[]{:S(2)}, u32[]{:S(2)}) collective-permute-start(bf16[8,1536]{1,0:T(8,128)(2,1)S(1)} %get-tuple-element.13), channel_id=1, source_target_pairs={{0,3},{1,2},{2,1},{3,0},{4,7},{5,6},{6,5},{7,4},{8,11},{9,10},{10,... | collective-permute-start | bytes 73736 | tf_op jit(solution)/shard_map/ppermute | solution.py:40
  19.3 0.6 %collective-permute-start.7 = (bf16[8,1536]{1,0:T(8,128)(2,1)S(1)}, bf16[8,1536]{1,0:T(8,128)(2,1)S(1)}, u32[]{:S(2)}, u32[]{:S(2)}) collective-permute-start(bf16[8,1536]{1,0:T(8,128)(2,1)S(1)} %get-tuple-element.14), channel_id=1, source_target_pairs={{0,2},{1,3},{2,0},{3,1},{4,6},{5,7},{6,4},{7,5},{8,10},{9,11},{10,... | collective-permute-start | bytes 73736 | tf_op jit(solution)/shard_map/ppermute | solution.py:40
  19.9 1.8 %collective-permute-start.8 = (bf16[8,1536]{1,0:T(8,128)(2,1)S(1)}, bf16[8,1536]{1,0:T(8,128)(2,1)S(1)}, u32[]{:S(2)}, u32[]{:S(2)}) collective-permute-start(bf16[8,1536]{1,0:T(8,128)(2,1)S(1)} %get-tuple-element.15), channel_id=1, source_target_pairs={{0,1},{1,0},{2,3},{3,2},{4,5},{5,4},{6,7},{7,6},{8,9},{9,8},{10,11... | collective-permute-start | bytes 73736 | tf_op jit(solution)/shard_map/ppermute | solution.py:40
  21.7 1.3 %collective-permute-done.6.refs_0_ = bf16[8,1536]{1,0:T(8,128)(2,1)S(1)} collective-permute-done((bf16[8,1536]{1,0:T(8,128)(2,1)S(1)}, bf16[8,1536]{1,0:T(8,128)(2,1)S(1)}, u32[]{:S(2)}, u32[]{:S(2)}) %collective-permute-start.6) | collective-permute-done | bytes 24608 | tf_op jit(solution)/shard_map/ppermute | solution.py:40
  23.1 1.0 %collective-permute-done.7.refs_1_ = bf16[8,1536]{1,0:T(8,128)(2,1)S(1)} collective-permute-done((bf16[8,1536]{1,0:T(8,128)(2,1)S(1)}, bf16[8,1536]{1,0:T(8,128)(2,1)S(1)}, u32[]{:S(2)}, u32[]{:S(2)}) %collective-permute-start.7) | collective-permute-done | bytes 24608 | tf_op jit(solution)/shard_map/ppermute | solution.py:40
  24.0 0.0 collective-permute-done.8.refs_2_
  24.0 0.6 %second_term.1 = (bf16[8,1536]{1,0:T(8,128)(2,1)}, bf16[8,1536]{1,0:T(8,128)(2,1)}) custom-call(bf16[8,1536]{1,0:T(8,128)(2,1)S(1)} %collective-permute-done.6.refs_0_, bf16[8,1536]{1,0:T(8,128)(2,1)S(1)} %collective-permute-done.7.refs_1_, bf16[8,1536]{1,0:T(8,128)(2,1)S(1)} %collective-permute-done.8.refs_2_, ...), custom_call_target="tpu_custom_call" | custom-call | tf_op jit(solution)/shard_map/second_term/pallas_call | solution.py:195
Async XLA Ops:
  0.6 9.5 %collective-permute-start = (bf16[8,1536]{1,0:T(8,128)(2,1)}, bf16[8,1536]{1,0:T(8,128)(2,1)S(1)}, u32[]{:S(2)}, u32[]{:S(2)}) collective-permute-start(bf16[8,1536]{1,0:T(8,128)(2,1)} %bitcast.4), channel_id=1, source_target_pairs={{0,1},{1,3},{2,0},{3,2},{4,5},{5,7},{6,4},{7,6},{8,9},{9,11},{10,8... | collective-permute-start | bytes 73736 | tf_op jit(solution)/shard_map/ppermute | solution.py:40
  3.7 6.4 %collective-permute-start.1 = (bf16[8,1536]{1,0:T(8,128)(2,1)}, bf16[8,1536]{1,0:T(8,128)(2,1)S(1)}, u32[]{:S(2)}, u32[]{:S(2)}) collective-permute-start(bf16[8,1536]{1,0:T(8,128)(2,1)} %bitcast.5), channel_id=1, source_target_pairs={{0,3},{1,2},{2,1},{3,0},{4,7},{5,6},{6,5},{7,4},{8,11},{9,10},{10,... | collective-permute-start | bytes 73736 | tf_op jit(solution)/shard_map/ppermute | solution.py:40
  6.2 4.0 %collective-permute-start.2 = (bf16[8,1536]{1,0:T(8,128)(2,1)}, bf16[8,1536]{1,0:T(8,128)(2,1)S(1)}, u32[]{:S(2)}, u32[]{:S(2)}) collective-permute-start(bf16[8,1536]{1,0:T(8,128)(2,1)} %bitcast.6), channel_id=1, source_target_pairs={{0,2},{1,0},{2,3},{3,1},{4,6},{5,4},{6,7},{7,5},{8,10},{9,8},{10,1... | collective-permute-start | bytes 73736 | tf_op jit(solution)/shard_map/ppermute | solution.py:40
  7.8 2.5 %copy-start = (f32[1,6144]{1,0:T(1,128)S(1)}, f32[1,6144]{1,0:T(1,128)}, u32[]{:S(2)}) copy-start(f32[1,6144]{1,0:T(1,128)} %refs_6_.3) | copy-start | bytes 73732
  7.8 2.5 %copy-start.1 = (bf16[8,1,1,1536]{3,0,2,1:T(8,128)(2,1)S(1)}, bf16[8,1,1,1536]{3,0,2,1:T(8,128)(2,1)}, u32[]{:S(2)}) copy-start(bf16[8,1,1,1536]{3,0,2,1:T(8,128)(2,1)} %param.6) | copy-start | bytes 73732
  7.8 2.5 %copy-start.2 = (s32[1,1,8]{2,1,0:T(1,128)S(1)}, s32[1,1,8]{2,1,0:T(1,128)}, u32[]{:S(2)}) copy-start(s32[1,1,8]{2,1,0:T(1,128)} %refs_3_.1) | copy-start | bytes 100
  7.8 2.5 %copy-start.3 = (s32[1,1,8]{2,1,0:T(1,128)S(1)}, s32[1,1,8]{2,1,0:T(1,128)}, u32[]{:S(2)}) copy-start(s32[1,1,8]{2,1,0:T(1,128)} %refs_4_.1) | copy-start | bytes 100
  10.8 4.7 %collective-permute-start.4 = (bf16[8,6144]{1,0:T(8,128)(2,1)S(1)}, bf16[8,6144]{1,0:T(8,128)(2,1)S(1)}, u32[]{:S(2)}, u32[]{:S(2)}) collective-permute-start(bf16[8,6144]{1,0:T(8,128)(2,1)S(1)} %first_product.1.refs_0_), channel_id=1, source_target_pairs={{0,8},{4,12},{8,0},{12,4},{1,9},{5,13},{9,1},{13,5},{2,10},{6,14},... | collective-permute-start | bytes 294920 | tf_op jit(solution)/shard_map/ppermute | solution.py:49
  12.3 3.1 %collective-permute-start.3 = (bf16[8,6144]{1,0:T(8,128)(2,1)S(1)}, bf16[8,6144]{1,0:T(8,128)(2,1)S(1)}, u32[]{:S(2)}, u32[]{:S(2)}) collective-permute-start(bf16[8,6144]{1,0:T(8,128)(2,1)S(1)} %first_product.1.refs_0_), channel_id=1, source_target_pairs={{0,4},{4,0},{8,12},{12,8},{1,5},{5,1},{9,13},{13,9},{2,6},{6,2},{1... | collective-permute-start | bytes 294920 | tf_op jit(solution)/shard_map/ppermute | solution.py:50
  15.4 1.3 %collective-permute-start.5 = (bf16[8,6144]{1,0:T(8,128)(2,1)S(1)}, bf16[8,6144]{1,0:T(8,128)(2,1)S(1)}, u32[]{:S(2)}, u32[]{:S(2)}) collective-permute-start(bf16[8,6144]{1,0:T(8,128)(2,1)S(1)} %collective-permute-done.4.refs_2_), channel_id=1, source_target_pairs={{0,4},{4,0},{8,12},{12,8},{1,5},{5,1},{9,13},{13,9},{2,6},{6,2},{1... | collective-permute-start | bytes 294920 | tf_op jit(solution)/shard_map/ppermute | solution.py:50
  17.3 5.8 %collective-permute-start.6 = (bf16[8,1536]{1,0:T(8,128)(2,1)S(1)}, bf16[8,1536]{1,0:T(8,128)(2,1)S(1)}, u32[]{:S(2)}, u32[]{:S(2)}) collective-permute-start(bf16[8,1536]{1,0:T(8,128)(2,1)S(1)} %get-tuple-element.13), channel_id=1, source_target_pairs={{0,3},{1,2},{2,1},{3,0},{4,7},{5,6},{6,5},{7,4},{8,11},{9,10},{10,... | collective-permute-start | bytes 73736 | tf_op jit(solution)/shard_map/ppermute | solution.py:40
  19.3 4.7 %collective-permute-start.7 = (bf16[8,1536]{1,0:T(8,128)(2,1)S(1)}, bf16[8,1536]{1,0:T(8,128)(2,1)S(1)}, u32[]{:S(2)}, u32[]{:S(2)}) collective-permute-start(bf16[8,1536]{1,0:T(8,128)(2,1)S(1)} %get-tuple-element.14), channel_id=1, source_target_pairs={{0,2},{1,3},{2,0},{3,1},{4,6},{5,7},{6,4},{7,5},{8,10},{9,11},{10,... | collective-permute-start | bytes 73736 | tf_op jit(solution)/shard_map/ppermute | solution.py:40
  19.9 4.1 %collective-permute-start.8 = (bf16[8,1536]{1,0:T(8,128)(2,1)S(1)}, bf16[8,1536]{1,0:T(8,128)(2,1)S(1)}, u32[]{:S(2)}, u32[]{:S(2)}) collective-permute-start(bf16[8,1536]{1,0:T(8,128)(2,1)S(1)} %get-tuple-element.15), channel_id=1, source_target_pairs={{0,1},{1,0},{2,3},{3,2},{4,5},{5,4},{6,7},{7,6},{8,9},{9,8},{10,11... | collective-permute-start | bytes 73736 | tf_op jit(solution)/shard_map/ppermute | solution.py:40
